TPU v7x, 32 devices: a whole 2x2x4 slice. The times are simulated.
32 devices in a mesh: member: 2 (over x), slab: 16 (over z, y, core).
Axes of the slice: x: 2, y: 2, z: 4, core: 2. Of those that a mesh axis runs over, the one named last changes fastest.
Arguments:
- prior_ensemble_fields: float32 [64, 6, 128, 1, 1024], P('member', None, 'slab'), may hold values from -6 to 6
- params: float32 [64, 12], P('member'), may hold values from -3 to 3
- influence: int32 [12, 6], replicated, may hold values 0 or 1
- obs_cell: int32 [128, 2, 128], P('slab', 'member'), may hold values from 0 to 3071
- obs_value: float32 [128, 2, 128], P('slab', 'member'), may hold values from -6 to 6
- obs_prec: float32 [128, 2, 128], P('slab', 'member'), may hold values from 0.5 to 4
- cutoff: int32 [128], P('slab'), may hold values from 4 to 8, as said below
Outputs:
- analysis: bfloat16 [64, 6, 128, 1, 1024], P('member', None, 'slab')
- param_analysis: float32 [64, 12], P('member')
Inputs may be any that keep to these rules, and one draw needn't show every extreme that they name: `obs_cell`: index = field * 512 + level * 512 + column within the block. `cutoff`: 8 is reached by some rows.
All inputs are finite; a program needn't handle non-finite values.
Results may differ from a plain program's by a relative error of at most 0.0056.
Values may be sent and summed in bfloat16 or wider, within the bound.
No kernel may reach another device: no remote copies, remote signals or barrier semaphores. Data moves between devices by JAX's collectives and lax.ppermute only.
A program may use at most 128 MiB of HBM per device.

v0:
```python
import math

import jax
import jax.numpy as jnp
from jax import lax
from jax.experimental import pallas as pl
from jax.experimental.pallas import tpu as pltpu
from jax.sharding import PartitionSpec as P


HALO = 8
STEPS = 4
NS_STEPS = 5
LANES = 128
TILE = 8
PACE = 4
HEAD = 1
KERNEL_VMEM = 44 * 1024 * 1024

diffusion = 0.2
advection = 0.15
vertical = 0.1
coupling = 0.2


def planes_of(fields, levels):
    return [(f, l) for f in range(fields) for l in range(levels)]


def place_in_pair():
    return lax.axis_index("slab") % 2


def pack_kernel(fields, rows, levels, cols, count, keep, x_ref, *rest):
    outs, edges, sems = rest[:2 * count + 1], *rest[2 * count + 1:2 * count + 3]
    turned = outs[-1] if keep else rest[-1]
    groups = cols // LANES
    stride = fields * rows * levels * groups
    planes = fields * levels
    tile = pl.program_id(0)

    def row(y, _):
        for p, (f, l) in enumerate(planes_of(fields, levels)):
            for s in range(groups):
                start = ((f * rows + y) * levels + l) * groups + s
                turned[tile, p, y, :, s * LANES:(s + 1) * LANES] = x_ref[pl.ds(start, TILE, stride=stride), :]
        return 0

    lax.fori_loop(0, rows, row, 0)

    def edge(y, _):
        for side in range(2):
            at = jnp.where(place_in_pair() == side, rows - STEPS, 0) + y
            for p in range(planes):
                edges[tile, side, p, y] = turned[tile, p, at].astype(jnp.bfloat16)
        return 0

    lax.fori_loop(0, STEPS, edge, 0)

    def copies(k):
        pairs = [(edges.at[k, 0], outs[2 * k]), (edges.at[k, 1], outs[2 * k + 1])]
        if not keep:
            pairs.append((turned.at[k], outs[-1].at[k]))
        return [pltpu.make_async_copy(src, dst, sems.at[k, i]) for i, (src, dst) in enumerate(pairs)]

    for k in range(count):
        @pl.when(tile == k)
        def _():
            for copy in copies(k):
                copy.start()

    @pl.when(tile == count - 1)
    def _():
        for k in range(count):
            for copy in copies(k):
                copy.wait()


def pack(x2, first, count, keep, fields, rows, levels, cols):
    limit = {"vmem_limit_bytes": KERNEL_VMEM} if keep else {}
    planes = fields * levels
    block = TILE * fields * rows * levels * cols // LANES
    edge = (planes, STEPS, TILE, cols)
    turned = (count, planes, rows, TILE, cols)
    return pl.pallas_call(
        lambda *refs: pack_kernel(fields, rows, levels, cols, count, keep, *refs),
        grid=(count,),
        in_specs=[pl.BlockSpec((block, LANES), lambda i: (first + i, 0))],
        out_specs=[pl.BlockSpec(memory_space=pltpu.HBM)] * (2 * count)
        + [pl.BlockSpec(memory_space=pltpu.VMEM if keep else pltpu.HBM)],
        out_shape=[jax.ShapeDtypeStruct(edge, jnp.bfloat16)] * (2 * count)
        + [pltpu.VMEM(turned, jnp.float32) if keep else jax.ShapeDtypeStruct(turned, jnp.float32)],
        scratch_shapes=[
            pltpu.VMEM((count, 2, *edge), jnp.bfloat16),
            pltpu.SemaphoreType.DMA((count, 3)),
        ]
        + ([] if keep else [pltpu.VMEM(turned, jnp.float32)]),
        compiler_params=pltpu.CompilerParams(**limit),
        name="pack",
    )(pltpu.with_memory_space_constraint(x2, pltpu.HBM))


def stencil_kernel(fields, rows, levels, cols, blocks, splits, local, held, x_ref, first_ref, second_ref, coef_ref, *rest):
    small_refs, rest = rest[:blocks], rest[blocks + held:]
    out_refs = rest[:len(splits)]
    obs_ref = rest[len(splits)]
    *state, mixed, sem = rest[len(splits) + 1:]
    groups = cols // LANES
    block_cols = cols // blocks
    pairs = planes_of(fields, levels)
    planes = len(pairs)

    own_copy = pltpu.make_async_copy(x_ref.at[local], state[0].at[:, pl.ds(STEPS, rows)], sem)
    own_copy.start()

    def tile_at(s):
        return slice(s * LANES, (s + 1) * LANES)

    odd = place_in_pair() == 1

    def load_edge(y, _):
        for p in range(planes):
            first = first_ref[p, y].astype(jnp.float32)
            second = second_ref[p, y].astype(jnp.float32)
            state[0][p, y] = jnp.where(odd, first, second)
            state[0][p, STEPS + rows + y] = jnp.where(odd, second, first)
        return 0

    lax.fori_loop(0, STEPS, load_edge, 0)
    own_copy.wait()
    place = lax.axis_index("slab")
    is_open = [jnp.where(place > 0, 1.0, 0.0), jnp.where(place < lax.axis_size("slab") - 1, 1.0, 0.0)]

    lane = lax.broadcasted_iota(jnp.int32, (TILE, LANES), 1)
    at_last = lane == LANES - 1
    at_first = lane == 0
    centre = (1.0 - 4.0 * diffusion - vertical) / diffusion
    below_part = vertical / diffusion
    right_part = (diffusion - advection) / diffusion
    left_part = (diffusion + advection) / diffusion
    next_part = coupling / diffusion
    scale = diffusion ** STEPS
    coefs = [jnp.broadcast_to(next_part * coef_ref[:, f:f + 1], (TILE, LANES)) for f in range(fields)]

    def rest_of_step(src, y, p):
        f, l = pairs[p]
        after = ((f + 1) % fields) * levels + l
        under = f * levels + (l - 1) % levels
        mid, out = [], []
        for s in range(groups):
            here = src[p, y, :, tile_at(s)]
            around = src[p, y + 1, :, tile_at(s)] + src[p, y - 1, :, tile_at(s)]
            if under == p:
                whole = centre + below_part
                own = here if abs(whole - 1.0) < 1e-12 else whole * here
            else:
                own = centre * here + below_part * src[under, y, :, tile_at(s)]
            mid.append(here)
            out.append((around + own) + coefs[f] * src[after, y, :, tile_at(s)])
        return mid, out

    def shifted(tiles):
        moved = []
        for s in range(0, groups, 2):
            both = jnp.concatenate(tiles[s:s + 2], axis=0).astype(jnp.bfloat16)
            both = pltpu.roll(both, LANES - 1, 1).astype(jnp.float32)
            moved += [both[k:k + TILE] for k in range(0, both.shape[0], TILE)]
        return moved

    pace = PACE if rows % PACE == 0 else 1
    for t in range(1, STEPS + 1):
        src, dst = state[(t - 1) % 2], state[t % 2]
        reach = STEPS - t
        ratio = math.comb(STEPS, t - 1) / math.comb(STEPS, t)

        def edge_rows(i, _):
            for side, y in enumerate((t + i, STEPS + rows + i)):
                for p in range(planes):
                    for s, value in enumerate(rest_of_step(src, y, p)[1]):
                        dst[p, y, :, tile_at(s)] = value * is_open[side]
            return 0

        def own_rows(i, _):
            for k in range(pace):
                mine = pace * i + k
                for p in range(planes):
                    mid, out = rest_of_step(src, STEPS + mine, p)
                    if t > 1:
                        mid = [mixed[p, mine, :, tile_at(s)] for s in range(groups)]
                    ahead = shifted(mid)
                    behind = [pltpu.roll(v, 1, 1) for v in mid]
                    for s in range(groups):
                        right = jnp.where(at_last, ahead[(s + 1) % groups], ahead[s])
                        left = jnp.where(at_first, behind[(s - 1) % groups], behind[s])
                        value = out[s] + (ratio * right_part * right + ratio * left_part * left)
                        if t < STEPS:
                            dst[p, STEPS + mine, :, tile_at(s)] = out[s]
                            mixed[p, mine, :, tile_at(s)] = value
                            continue
                        value = value * scale
                        mixed[p, mine, :, tile_at(s)] = value
                        for g, (start, count) in enumerate(splits):
                            if start <= p < start + count:
                                at = pl.ds(pl.multiple_of(mine * TILE, TILE), TILE)
                                out_refs[g][p - start, s, at, :] = value.astype(jnp.bfloat16)
            return 0

        if reach:
            lax.fori_loop(0, reach, edge_rows, 0)
        lax.fori_loop(0, rows // pace, own_rows, 0)

    column = lax.broadcasted_iota(jnp.int32, (block_cols, LANES), 0)

    def observe(i, _):
        for k in range(pace):
            y = pace * i + k
            for b in range(blocks):
                cell = small_refs[b][pl.ds(y, 1), :].astype(jnp.int32)
                plane = cell // block_cols
                pick = jnp.where(column == cell - plane * block_cols, 1.0, 0.0).astype(jnp.bfloat16)
                start = (lax.axis_index("member") + b) % blocks * block_cols
                part = mixed[:, y, :, pl.ds(pl.multiple_of(start, LANES), block_cols)]
                part = part.reshape(planes * TILE, block_cols).astype(jnp.bfloat16)
                found = jnp.dot(part, pick, preferred_element_type=jnp.float32).reshape(planes, TILE, LANES)
                total = jnp.zeros((TILE, LANES), jnp.float32)
                for p in range(planes):
                    total = jnp.where(plane == p, found[p], total)
                obs_ref[0, y, b] = total.astype(jnp.bfloat16)
        return 0

    lax.fori_loop(0, rows // pace, observe, 0)


def stencil(turned, first, second, coef, smalls, held, tile, local, splits, fields, rows, levels, cols):
    planes = fields * levels
    blocks = len(smalls)
    tiles = coef.shape[0] // TILE
    outs = [jax.ShapeDtypeStruct((count, cols // LANES, rows * TILE, LANES), jnp.bfloat16) for _, count in splits]
    observed = jax.ShapeDtypeStruct((tiles, rows, blocks, TILE, LANES), jnp.bfloat16)
    room = pltpu.VMEM((planes, rows + 2 * STEPS, TILE, cols), jnp.float32)
    far = pl.BlockSpec(memory_space=pltpu.HBM)

    near = pl.BlockSpec(memory_space=pltpu.VMEM)
    in_specs = [near if tile < HEAD else far, near, near, pl.BlockSpec((TILE, fields), lambda i: (tile, 0))]
    in_specs += [near] * len(smalls)
    args = [turned, first, second, coef, *(near_core(small) for small in smalls)]
    aliases = {}
    if held is not None:
        aliases = {len(args): len(splits)}
        in_specs.append(far)
        args.append(held)
    return pl.pallas_call(
        lambda *refs: stencil_kernel(fields, rows, levels, cols, blocks, splits, local, len(aliases), *refs),
        grid=(1,),
        in_specs=in_specs,
        out_specs=[pl.BlockSpec(out.shape, lambda i: (0, 0, 0, 0)) for out in outs]
        + [pl.BlockSpec((1, *observed.shape[1:]), lambda i: (tile, 0, 0, 0, 0))],
        out_shape=[*outs, observed],
        scratch_shapes=[
            room,
            room,
            pltpu.VMEM((planes, rows, TILE, cols), jnp.float32),
            pltpu.SemaphoreType.DMA,
        ],
        input_output_aliases=aliases,
        compiler_params=pltpu.CompilerParams(vmem_limit_bytes=KERNEL_VMEM),
        name="stencil",
    )(*args)


def product(a, b):
    a_high = a.astype(jnp.bfloat16)
    a_low = (a - a_high.astype(jnp.float32)).astype(jnp.bfloat16)
    b_high = b.astype(jnp.bfloat16)
    b_low = (b - b_high.astype(jnp.float32)).astype(jnp.bfloat16)
    left = jnp.concatenate([a_high, a_low], axis=1)
    right = jnp.concatenate(
        [jnp.concatenate([b_high, b_low], axis=1), jnp.concatenate([b_high, jnp.zeros_like(b_low)], axis=1)], axis=0
    )
    both = jnp.dot(left, right, preferred_element_type=jnp.float32)
    return both[:, :b.shape[1]] + both[:, b.shape[1]:]


def solve_kernel(rows, members, ensemble, pairs, table_ref, own_ref, near_ref, far_ref, upper_ref, lower_ref, sum_ref, wide, ys, zs, ms, gs, scales, direct):
    width = 2 * ensemble
    count = rows * pairs
    odd = place_in_pair() == 1

    def fill(r, _):
        for q in range(pairs):
            near = near_ref[r, q].astype(jnp.float32)
            far = far_ref[r, q].astype(jnp.float32)
            wide[r, q] = jnp.where(odd, near, far)
            wide[rows + r, q] = own_ref[r, q]
            wide[2 * rows + r, q] = jnp.where(odd, far, near)
        return 0

    lax.fori_loop(0, rows, fill, 0)

    lane = lax.broadcasted_iota(jnp.int32, (ensemble, width), 1)
    first = lane < ensemble
    eye = jnp.where(
        lax.broadcasted_iota(jnp.int32, (width, width), 0) == lax.broadcasted_iota(jnp.int32, (width, width), 1), 1.0, 0.0
    )
    first_row = lax.broadcasted_iota(jnp.int32, (TILE, width), 1) < ensemble

    def localize(i, _):
        for y, q in ((2 * i + k, q) for k in range(2) for q in range(pairs)):
            local = jnp.zeros(wide.shape[2:], jnp.float32)
            for d in range(-HALO, HALO + 1):
                local = local + table_ref[d + HALO, y] * wide[rows + y + d, q]
            gram = local[:ensemble]
            amat = jnp.concatenate([jnp.where(first, gram, 0.0), jnp.where(first, 0.0, gram)], axis=0) + (ensemble - 1.0) * eye
            square = amat * amat
            tops = jnp.sqrt(jnp.sum(square[:ensemble], axis=(0, 1), keepdims=True))
            ends = jnp.sqrt(jnp.sum(square[ensemble:], axis=(0, 1), keepdims=True))
            part = jnp.concatenate(
                [jnp.broadcast_to(1.0 / tops, (ensemble, width)), jnp.broadcast_to(1.0 / ends, (ensemble, width))], axis=0
            )
            at = y * pairs + q
            ys[at] = amat * part
            gs[at] = local[ensemble:ensemble + TILE]
            scales[at] = jnp.where(first_row, tops, ends)
        return 0

    lax.fori_loop(0, rows // 2, localize, 0)

    pace = 8 if count % 8 == 0 else 1

    def each(work):
        def some(i, _):
            for k in range(pace):
                work(pace * i + k)
            return 0

        lax.fori_loop(0, count // pace, some, 0)

    for step_idx in range(NS_STEPS):
        def middle(i):
            ms[i] = 1.5 * eye - 0.5 * (product(zs[i], ys[i]) if step_idx else ys[i])

        def apply(i):
            if step_idx < NS_STEPS - 1:
                ys[i] = product(ys[i], ms[i])
            zs[i] = product(ms[i], zs[i]) if step_idx else ms[i]

        each(middle)
        each(apply)

    def weigh(i, total):
        for y, q in ((2 * i + k, q) for k in range(2) for q in range(pairs)):
            at = y * pairs + q
            z, scale = zs[at], scales[at]
            mean = (product(product(gs[at], z), z) / scale)[:1]
            wpert = z[:members] + z[ensemble:ensemble + members]
            weights = wpert * (math.sqrt(ensemble - 1.0) / jnp.sqrt(scale))[:1] + mean
            total = total + weights
            here = first[:members]
            low = jnp.sum(jnp.where(here, weights, 0.0), axis=1, keepdims=True)
            high = jnp.sum(jnp.where(here, 0.0, weights), axis=1, keepdims=True)
            direct[q, pl.ds(y, members, stride=rows), :] = weights + (1.0 - jnp.where(here, low, high)) / ensemble
        return total

    sum_ref[...] = lax.fori_loop(0, rows // 2, weigh, jnp.zeros((members, width), jnp.float32))

    depth = ensemble * rows
    column = lax.broadcasted_iota(jnp.int32, (width, depth), 1)
    member = column // (rows * TILE) * TILE + column % TILE
    entry = lax.broadcasted_iota(jnp.int32, (width, depth), 0)
    mine = lax.broadcasted_iota(jnp.int32, (members * rows, depth), 0) % rows
    theirs = lax.broadcasted_iota(jnp.int32, (members * rows, depth), 1) // TILE % rows
    keep = mine == theirs
    for half in range(2):
        place = jnp.where(entry == member + half * ensemble, 1.0, 0.0).astype(jnp.bfloat16)
        for q in range(pairs):
            w = direct[q]
            high = w.astype(jnp.bfloat16)
            low = (w - high.astype(jnp.float32)).astype(jnp.bfloat16)
            for part, ref in ((high, upper_ref), (low, lower_ref)):
                spread = jnp.dot(part, place, preferred_element_type=jnp.float32)
                ref[2 * q + half] = jnp.where(keep, spread, 0.0).astype(jnp.bfloat16)


def solve(table, own, near, far, members, ensemble):
    rows, pairs, tall, width = own.shape
    count = rows * pairs
    out = pltpu.VMEM((2 * pairs, members * rows, ensemble * rows), jnp.bfloat16)
    square = pltpu.VMEM((count, width, width), jnp.float32)
    line = pltpu.VMEM((count, TILE, width), jnp.float32)
    smem = pl.BlockSpec(memory_space=pltpu.SMEM)
    vmem = pl.BlockSpec(memory_space=pltpu.VMEM)
    return pl.pallas_call(
        lambda *refs: solve_kernel(rows, members, ensemble, pairs, *refs),
        in_specs=[smem, vmem, vmem, vmem],
        out_specs=[vmem] * 3,
        out_shape=[out, out, jax.ShapeDtypeStruct((members, width), jnp.float32)],
        scratch_shapes=[
            pltpu.VMEM((3 * rows, pairs, tall, width), jnp.float32),
            square, square, square, line, line,
            pltpu.VMEM((pairs, members * rows, width), jnp.float32),
        ],
        compiler_params=pltpu.CompilerParams(vmem_limit_bytes=KERNEL_VMEM),
        name="solve",
    )(table, own, near, far)


def update_kernel(members, rows, cols, blocks, offsets, upper, lower, *rest):
    pieces, out_ref = rest[:len(offsets)], rest[-1]
    plane, b = pl.program_id(0), pl.program_id(1)
    groups = cols // blocks // LANES
    columns = []
    for s in range(groups):
        columns.append(jnp.concatenate([piece[at + plane, b * groups + s] for piece, at in zip(pieces, offsets)], axis=0))
    x = jnp.concatenate(columns, axis=1) if groups > 1 else columns[0]
    mine = (b + blocks - lax.axis_index("member")) % blocks
    total = jnp.dot(upper[mine], x, preferred_element_type=jnp.float32)
    total = total + jnp.dot(lower[mine], x, preferred_element_type=jnp.float32)
    out_ref[:, 0] = total.reshape(members, rows, groups * LANES).astype(jnp.bfloat16)


def update(upper, lower, pieces, offsets, start, count, held, members, planes, rows, cols):
    blocks = upper.shape[0]
    in_specs = [pl.BlockSpec(memory_space=pltpu.VMEM)] * (2 + len(pieces))
    args = [upper, lower, *(near_core(piece) for piece in pieces)]
    aliases = {}
    if held is not None:
        aliases = {len(args): 0}
        in_specs.append(pl.BlockSpec(memory_space=pl.ANY))
        args.append(held)
    return pl.pallas_call(
        lambda *refs: update_kernel(members, rows, cols, blocks, offsets, *refs),
        grid=(count, blocks),
        in_specs=in_specs,
        out_specs=pl.BlockSpec((members, 1, rows, cols // blocks), lambda i, b: (0, start + i, 0, b)),
        out_shape=jax.ShapeDtypeStruct((members, planes, rows, cols), jnp.bfloat16),
        input_output_aliases=aliases,
        compiler_params=pltpu.CompilerParams(vmem_limit_bytes=KERNEL_VMEM),
        name="update",
    )(*args)


def near_core(array):
    return pltpu.with_memory_space_constraint(array, pltpu.VMEM)


def from_member(array, shift):
    count = lax.axis_size("member")
    return lax.ppermute(array, "member", [((i + shift) % count, i) for i in range(count)])


def all_members(array):
    return [array] + [from_member(array, shift) for shift in range(1, lax.axis_size("member"))]


def swap_one(array):
    return lax.ppermute(array, "slab", [(i, i ^ 1) for i in range(lax.axis_size("slab"))])


def swap_two(array):
    pairs = [(i, i + 1) for i in range(1, lax.axis_size("slab") - 1, 2)]
    return lax.ppermute(array, "slab", pairs + [(j, i) for i, j in pairs])


def groups_of(planes):
    sizes = [2] * (planes // 2 - 1) + [1, 1] if planes % 2 == 0 else [1] * planes
    return [(sum(sizes[:i]), size) for i, size in enumerate(sizes)]


def cycle(prior_ensemble_fields, params, influence, obs_cell, obs_value, obs_prec, cutoff):
    highest = lax.Precision.HIGHEST
    fine_grain = lax.Precision.HIGH
    members, fields, rows, levels, cols = prior_ensemble_fields.shape
    planes = fields * levels
    tiles = members // TILE
    devices = lax.axis_size("member")
    slabs = lax.axis_size("slab")
    ensemble = members * devices
    dims = (fields, rows, levels, cols)
    x2 = prior_ensemble_fields.reshape(members * fields * rows * levels * (cols // LANES), LANES)

    head = min(HEAD, tiles)
    *packed, turned = pack(x2, 0, head, True, *dims)
    turned = [(turned, i) for i in range(head)]
    if tiles > head:
        *more, others = pack(x2, head, tiles - head, False, *dims)
        packed += more
        others = pltpu.with_memory_space_constraint(others, pltpu.HBM)
        turned += [(others, i) for i in range(tiles - head)]
    edges = []
    for i in range(tiles):
        edges.append((near_core(swap_one(packed[2 * i])), near_core(swap_two(packed[2 * i + 1]))))

    columns = obs_cell.shape[2]
    npar = params.shape[1]
    own_small = jnp.concatenate(
        [obs_cell[:, 0].astype(jnp.float32), obs_value[:, 0], obs_prec[:, 0]]
        + [jnp.pad(params.T, ((0, -npar % TILE), (0, columns - members)))]
    )
    smalls = all_members(own_small)
    every_param = jnp.concatenate([small[3 * rows:3 * rows + npar, :members].T for small in smalls])
    values = jnp.stack([small[rows:2 * rows] for small in smalls], axis=1)
    precs = jnp.stack([small[2 * rows:3 * rows] for small in smalls], axis=1)

    coef = jnp.dot(params, influence.astype(jnp.float32), precision=highest)

    fine = groups_of(planes)
    forecasts, own_obs = [], None
    for i in range(tiles):
        splits = [(0, planes)]
        if i == tiles - 1:
            splits = fine
        elif i == 1:
            splits = [(0, fine[-2][0]), (fine[-2][0], planes - fine[-2][0])]
        fields_here, local = turned[i]
        *outs, own_obs = stencil(fields_here, *edges[i], coef, smalls, own_obs, i, local, splits, *dims)
        forecasts.append((splits, outs))
    ens_obs = jnp.stack([jnp.roll(array, shift, axis=2) for shift, array in enumerate(all_members(own_obs))])
    sent = []
    for splits, outs in forecasts:
        arrays = []
        for out in outs:
            arrays.append(all_members(out))
        sent.append((splits, arrays))

    ens_obs = ens_obs.transpose(2, 3, 0, 1, 4, 5).reshape(rows, devices, ensemble, LANES).astype(jnp.float32)
    ybar = jnp.mean(ens_obs, axis=2, keepdims=True)
    ypert = ens_obs - ybar
    weighted = precs * (values - ybar[:, :, 0])
    gram = jnp.einsum("rbeo,rbfo->rbef", ypert * precs[:, :, None], ypert, precision=fine_grain)
    gvec = jnp.einsum("rbeo,rbo->rbe", ypert, weighted, precision=highest)
    empty = jnp.zeros((rows, devices, TILE - 1, ensemble), jnp.float32)
    stacked = jnp.concatenate([gram, gvec[:, :, None, :], empty], axis=2)
    stacked = jnp.concatenate([stacked[:, 0::2], stacked[:, 1::2]], axis=3)
    rounded = stacked.astype(jnp.bfloat16)
    near, far = near_core(swap_one(rounded)), near_core(swap_two(rounded))
    radius = cutoff.astype(jnp.float32)
    distance = jnp.abs(jnp.arange(-HALO, HALO + 1, dtype=jnp.float32))[:, None]
    table = jnp.maximum(0.0, 1.0 - distance / (radius + 1.0))
    upper, lower, weight_rows = solve(table, near_core(stacked), near, far, members, ensemble)

    analysis = None
    for start, count in fine:
        pieces, offsets = [], []
        for r in range(devices):
            for splits, arrays in sent:
                part = max(k for k, (at, _) in enumerate(splits) if at <= start)
                pieces.append(arrays[part][r])
                offsets.append(start - splits[part][0])
        analysis = update(upper, lower, pieces, offsets, start, count, analysis, members, planes, rows, cols)
    analysis = analysis.reshape(members, fields, levels, rows, cols).transpose(0, 1, 3, 2, 4)

    pbar = jnp.mean(every_param, axis=0)
    ppert = every_param - pbar
    weight_rows = weight_rows[:, :ensemble] + weight_rows[:, ensemble:]
    part = jnp.einsum("jk,ej->ke", ppert, weight_rows, precision=highest)
    step = 1
    while step < slabs:
        part = part + lax.ppermute(part, "slab", [(i, i ^ step) for i in range(slabs)])
        step *= 2
    total = part / (rows * slabs * devices)
    param_analysis = pbar + total.T
    return (analysis, param_analysis)


def solution(mesh):
    in_specs = (
        P("member", None, "slab", None, None),
        P("member", None),
        P(),
        P("slab", "member", None),
        P("slab", "member", None),
        P("slab", "member", None),
        P("slab"),
    )
    out_specs = (P("member", None, "slab", None, None), P("member", None))
    return jax.shard_map(cycle, mesh=mesh, in_specs=in_specs, out_specs=out_specs, check_vma=False)
```

profile of v0, /device:TPU:17, one launch (start us, length us, event | category | flops | bytes accessed | tf_op | source)
XLA Modules:
  0.0 124.7 jit_solution(13159166172782919451)
XLA Ops:
  0.6 3.4 %pack.3 = (bf16[6,4,8,1024]{3,2,1,0:T(8,128)(2,1)}, bf16[6,4,8,1024]{3,2,1,0:T(8,128)(2,1)}, f32[1,6,8,8,1024]{4,3,2,1,0:T(8,128)S(1)}) custom-call(f32[12288,128]{1,0:T(8,128)} %bitcast.37), custom_call_target="tpu_custom_call" | custom-call | tf_op jit(solution)/shard_map/pack/pallas_call | solution.py:85
  4.1 0.7 collective-permute-start.7
  4.8 3.2 %collective-permute-start.8 = (bf16[6,4,8,1024]{3,2,1,0:T(8,128)(2,1)}, bf16[6,4,8,1024]{3,2,1,0:T(8,128)(2,1)S(1)}, u32[]{:S(2)}, u32[]{:S(2)}) collective-permute-start(bf16[6,4,8,1024]{3,2,1,0:T(8,128)(2,1)} %get-tuple-element.36), channel_id=1, source_target_pairs={{1,2},{3,4},{5,6},{7,8},{9,10},{11,12},{13,14},{2,1},{4,3},{6,5},{... | collective-permute-start | bytes 1179656 | tf_op jit(solution)/shard_map/ppermute | solution.py:461
  8.1 7.7 %pack.2 = (bf16[6,4,8,1024]{3,2,1,0:T(8,128)(2,1)}, bf16[6,4,8,1024]{3,2,1,0:T(8,128)(2,1)}, bf16[6,4,8,1024]{3,2,1,0:T(8,128)(2,1)}, bf16[6,4,8,1024]{3,2,1,0:T...) custom-call(f32[12288,128]{1,0:T(8,128)} %bitcast.38), custom_call_target="tpu_custom_call" | custom-call | tf_op jit(solution)/shard_map/pack/pallas_call | solution.py:85
  15.8 0.4 collective-permute-start.5
  16.2 1.3 %collective-permute-start.2 = (f32[40,128]{1,0:T(8,128)S(1)}, f32[40,128]{1,0:T(8,128)S(1)}, u32[]{:S(2)}, u32[]{:S(2)}) collective-permute-start(f32[40,128]{1,0:T(8,128)S(1)} %select_maximum_fusion.refs_4_), channel_id=1, source_target_pairs={{16,0},{0,16},{17,1},{1,17},{18,2},{2,18},{19,3},{3,19},{20,4},{4,... | collective-permute-start | bytes 61448 | tf_op jit(solution)/shard_map/ppermute | solution.py:448
  17.5 3.5 %collective-permute-start.6 = (bf16[6,4,8,1024]{3,2,1,0:T(8,128)(2,1)}, bf16[6,4,8,1024]{3,2,1,0:T(8,128)(2,1)S(1)}, u32[]{:S(2)}, u32[]{:S(2)}) collective-permute-start(bf16[6,4,8,1024]{3,2,1,0:T(8,128)(2,1)} %get-tuple-element.33), channel_id=1, source_target_pairs={{1,2},{3,4},{5,6},{7,8},{9,10},{11,12},{13,14},{2,1},{4,3},{6,5},{... | collective-permute-start | bytes 1179656 | tf_op jit(solution)/shard_map/ppermute | solution.py:461
  21.0 0.1 reduce_sum.30
  21.3 3.5 %collective-permute-start.4 = (bf16[6,4,8,1024]{3,2,1,0:T(8,128)(2,1)}, bf16[6,4,8,1024]{3,2,1,0:T(8,128)(2,1)S(1)}, u32[]{:S(2)}, u32[]{:S(2)}) collective-permute-start(bf16[6,4,8,1024]{3,2,1,0:T(8,128)(2,1)} %get-tuple-element.31), channel_id=1, source_target_pairs={{1,2},{3,4},{5,6},{7,8},{9,10},{11,12},{13,14},{2,1},{4,3},{6,5},{... | collective-permute-start | bytes 1179656 | tf_op jit(solution)/shard_map/ppermute | solution.py:461
  24.9 2.7 %collective-permute-start.1 = (bf16[6,4,8,1024]{3,2,1,0:T(8,128)(2,1)}, bf16[6,4,8,1024]{3,2,1,0:T(8,128)(2,1)S(1)}, u32[]{:S(2)}, u32[]{:S(2)}) collective-permute-start(bf16[6,4,8,1024]{3,2,1,0:T(8,128)(2,1)} %get-tuple-element.29), channel_id=1, source_target_pairs={{1,2},{3,4},{5,6},{7,8},{9,10},{11,12},{13,14},{2,1},{4,3},{6,5},{... | collective-permute-start | bytes 1179656 | tf_op jit(solution)/shard_map/ppermute | solution.py:461
  27.6 0.2 fusion.15.refs_3_
  27.9 4.4 %stencil.4 = (bf16[6,8,64,128]{3,2,1,0:T(8,128)(2,1)S(1)}, bf16[4,8,2,8,128]{4,3,2,1,0:T(8,128)(2,1)S(1)}) custom-call(f32[1,6,8,8,1024]{4,3,2,1,0:T(8,128)S(1)} %get-tuple-element.34.refs_0_, bf16[6,4,8,1024]{3,2,1,0:T(8,128)(2,1)S(1)} %collective-permute-done.7.refs_1_, bf16[6,4,8,1024]{3,2,1,0:T(8,128)(2,1)S(1)} %collective-permute-done.8.refs_2_, ...), custom_call_target="tpu_custom_call" | custom-call | tf_op jit(solution)/shard_map/stencil/pallas_call | solution.py:252
  32.2 7.2 %collective-permute-done.6.refs_2_ = bf16[6,4,8,1024]{3,2,1,0:T(8,128)(2,1)S(1)} collective-permute-done((bf16[6,4,8,1024]{3,2,1,0:T(8,128)(2,1)}, bf16[6,4,8,1024]{3,2,1,0:T(8,128)(2,1)S(1)}, u32[]{:S(2)}, u32[]{:S(2)}) %collective-permute-start.6) | collective-permute-done | bytes 393248 | tf_op jit(solution)/shard_map/ppermute | solution.py:461
  39.4 5.5 %stencil.5 = (bf16[4,8,64,128]{3,2,1,0:T(8,128)(2,1)S(1)}, bf16[2,8,64,128]{3,2,1,0:T(8,128)(2,1)S(1)}, bf16[4,8,2,8,128]{4,3,2,1,0:T(8,128)(2,1)S(1)}) custom-call(f32[3,6,8,8,1024]{4,3,2,1,0:T(8,128)} %get-tuple-element.27.refs_0_, bf16[6,4,8,1024]{3,2,1,0:T(8,128)(2,1)S(1)} %collective-permute-done.5.refs_1_, ...), custom_call_target="tpu_custom_call", output_to_operand_aliasing={{2}: (6, {})} | custom-call | tf_op jit(solution)/shard_map/stencil/pallas_call | solution.py:252
  45.0 5.5 %stencil.6 = (bf16[6,8,64,128]{3,2,1,0:T(8,128)(2,1)S(1)}, bf16[4,8,2,8,128]{4,3,2,1,0:T(8,128)(2,1)S(1)}) custom-call(f32[3,6,8,8,1024]{4,3,2,1,0:T(8,128)} %get-tuple-element.27.refs_0_, bf16[6,4,8,1024]{3,2,1,0:T(8,128)(2,1)S(1)} %collective-permute-done.3.refs_1_, ...), custom_call_target="tpu_custom_call", output_to_operand_aliasing={{1}: (6, {})} | custom-call | tf_op jit(solution)/shard_map/stencil/pallas_call | solution.py:252
  50.6 5.5 %stencil.7 = (bf16[2,8,64,128]{3,2,1,0:T(8,128)(2,1)S(1)}, bf16[2,8,64,128]{3,2,1,0:T(8,128)(2,1)S(1)}, bf16[1,8,64,128]{3,2,1,0:T(8,128)(2,1)S(1)}, bf16[1,8,64...) custom-call(f32[3,6,8,8,1024]{4,3,2,1,0:T(8,128)} %get-tuple-element.27.refs_0_, ...), custom_call_target="tpu_custom_call", output_to_operand_aliasing={{4}: (6, {})} | custom-call | tf_op jit(solution)/shard_map/stencil/pallas_call | solution.py:252
  56.1 0.3 collective-permute-start.9
  56.5 1.2 collective-permute-start.14
  57.7 0.3 collective-permute-start.17
  57.9 1.2 collective-permute-start.12
  59.1 2.6 %collective-permute-done.9 = bf16[4,8,2,8,128]{4,3,2,1,0:T(8,128)(2,1)S(1)} collective-permute-done((bf16[4,8,2,8,128]{4,3,2,1,0:T(8,128)(2,1)S(1)}, bf16[4,8,2,8,128]{4,3,2,1,0:T(8,128)(2,1)S(1)}, u32[]{:S(2)}, u32[]{:S(2)}) %collective-permute-start.9) | collective-permute-done | bytes 131104 | tf_op jit(solution)/shard_map/ppermute | solution.py:448
  62.1 0.5 fusion
  62.6 0.9 fusion.12
  63.5 0.1 maximum_maximum_fusion
  63.7 0.1 fusion.18
  64.0 0.3 collective-permute-start.19
  64.4 0.9 collective-permute-done.10.refs_2_
  65.3 4.3 %collective-permute-start.11 = (bf16[8,1,72,128]{3,2,1,0:T(8,128)(2,1)S(1)}, bf16[8,1,72,128]{3,2,1,0:T(8,128)(2,1)S(1)}, u32[]{:S(2)}, u32[]{:S(2)}) collective-permute-start(bf16[8,1,72,128]{3,2,1,0:T(8,128)(2,1)S(1)} %get-tuple-element.60), channel_id=1, source_target_pairs={{1,2},{3,4},{5,6},{7,8},{9,10},{11,12},{13,14},{2,1},{4,3},{6,5},{... | collective-permute-start | bytes 442376 | tf_op jit(solution)/shard_map/ppermute | solution.py:461
  69.6 4.4 %collective-permute-done.11.refs_3_ = bf16[8,1,72,128]{3,2,1,0:T(8,128)(2,1)S(1)} collective-permute-done((bf16[8,1,72,128]{3,2,1,0:T(8,128)(2,1)S(1)}, bf16[8,1,72,128]{3,2,1,0:T(8,128)(2,1)S(1)}, u32[]{:S(2)}, u32[]{:S(2)}) %collective-permute-start.11) | collective-permute-done | bytes 147488 | tf_op jit(solution)/shard_map/ppermute | solution.py:461
  74.0 5.9 %solve.1 = (bf16[2,256,512]{2,1,0:T(8,128)(2,1)S(1)}, bf16[2,256,512]{2,1,0:T(8,128)(2,1)S(1)}, f32[32,128]{1,0:T(8,128)S(1)}) custom-call(f32[17,8]{1,0:T(8,128)S(1)} %fusion.7.refs_0_, f32[8,1,72,128]{3,2,1,0:T(8,128)S(1)} %get-tuple-element.61.refs_1_, bf16[8,1,72,128]{3,2,1,0:T(8,128)(2,1)S(1)} %collective-permute-done.10.refs_2_, ...), custom_call_target="tpu_custom_call" | custom-call | tf_op jit(solution)/shard_map/solve/pallas_call | solution.py:392
  79.9 0.2 fusion.3
  80.1 1.2 collective-permute-done.20
  81.3 1.5 %collective-permute-start.21 = (f32[12,32]{1,0:T(8,128)S(1)}, f32[12,32]{1,0:T(8,128)S(1)}, u32[]{:S(2)}, u32[]{:S(2)}) collective-permute-start(f32[12,32]{1,0:T(8,128)S(1)} %add.42), channel_id=1, source_target_pairs={{0,2},{1,3},{2,0},{3,1},{4,6},{5,7},{6,4},{7,5},{8,10},{9,11},{10,... | collective-permute-start | bytes 4616 | tf_op jit(solution)/shard_map/ppermute | solution.py:558
  82.8 1.3 %collective-permute-done.21 = f32[12,32]{1,0:T(8,128)S(1)} collective-permute-done((f32[12,32]{1,0:T(8,128)S(1)}, f32[12,32]{1,0:T(8,128)S(1)}, u32[]{:S(2)}, u32[]{:S(2)}) %collective-permute-start.21) | collective-permute-done | bytes 1568 | tf_op jit(solution)/shard_map/ppermute | solution.py:558
  84.2 0.9 collective-permute-start.22
  85.1 1.9 %collective-permute-done.22 = f32[12,32]{1,0:T(8,128)S(1)} collective-permute-done((f32[12,32]{1,0:T(8,128)S(1)}, f32[12,32]{1,0:T(8,128)S(1)}, u32[]{:S(2)}, u32[]{:S(2)}) %collective-permute-start.22) | collective-permute-done | bytes 1568 | tf_op jit(solution)/shard_map/ppermute | solution.py:558
  87.0 21.7 %collective-permute-done.19.refs_9_ = bf16[2,8,64,128]{3,2,1,0:T(8,128)(2,1)S(1)} collective-permute-done((bf16[2,8,64,128]{3,2,1,0:T(8,128)(2,1)S(1)}, bf16[2,8,64,128]{3,2,1,0:T(8,128)(2,1)S(1)}, u32[]{:S(2)}, u32[]{:S(2)}) %collective-permute-start.19) | collective-permute-done | bytes 262176 | tf_op jit(solution)/shard_map/ppermute | solution.py:448
  108.7 0.3 collective-permute-start.18
  109.0 1.2 collective-permute-start.13
  110.2 0.3 collective-permute-start.16
  110.5 1.2 collective-permute-start.15
  111.7 0.7 add_bitcast_fusion
  112.3 2.8 %update.4.refs_10_ = bf16[32,6,8,1024]{3,2,1,0:T(8,128)(2,1)} custom-call(bf16[2,256,512]{2,1,0:T(8,128)(2,1)S(1)} %get-tuple-element.41.refs_0_, bf16[2,256,512]{2,1,0:T(8,128)(2,1)S(1)} %get-tuple-element.42.refs_1_, bf16[6,8,64,128]{3,2,1,0:T(8,128)(2,1)S(1)} %get-tuple-element.43.refs_2_, bf16[4,8,64,128]{3,2,1,0:T(8,128)(2,1)S(1)} %get-tuple-element.48.refs_3_, ...), custom_call_target="tpu_custom_call" | custom-call | tf_op jit(solution)/shard_map/update/pallas_call | solution.py:430
  115.1 1.9 %collective-permute-done.18.refs_9_ = bf16[2,8,64,128]{3,2,1,0:T(8,128)(2,1)S(1)} collective-permute-done((bf16[2,8,64,128]{3,2,1,0:T(8,128)(2,1)S(1)}, bf16[2,8,64,128]{3,2,1,0:T(8,128)(2,1)S(1)}, u32[]{:S(2)}, u32[]{:S(2)}) %collective-permute-start.18) | collective-permute-done | bytes 262176 | tf_op jit(solution)/shard_map/ppermute | solution.py:448
  117.0 2.8 %update.5.refs_10_ = bf16[32,6,8,1024]{3,2,1,0:T(8,128)(2,1)} custom-call(bf16[2,256,512]{2,1,0:T(8,128)(2,1)S(1)} %get-tuple-element.41.refs_0_, bf16[2,256,512]{2,1,0:T(8,128)(2,1)S(1)} %get-tuple-element.42.refs_1_, bf16[6,8,64,128]{3,2,1,0:T(8,128)(2,1)S(1)} %get-tuple-element.43.refs_2_, ...), custom_call_target="tpu_custom_call", output_to_operand_aliasing={{}: (10, {})} | custom-call | tf_op jit(solution)/shard_map/update/pallas_call | solution.py:430
  119.8 1.7 %collective-permute-done.16.refs_9_ = bf16[1,8,64,128]{3,2,1,0:T(8,128)(2,1)S(1)} collective-permute-done((bf16[1,8,64,128]{3,2,1,0:T(8,128)(2,1)S(1)}, bf16[1,8,64,128]{3,2,1,0:T(8,128)(2,1)S(1)}, u32[]{:S(2)}, u32[]{:S(2)}) %collective-permute-start.16) | collective-permute-done | bytes 131104 | tf_op jit(solution)/shard_map/ppermute | solution.py:448
  121.5 1.6 %update.6.refs_10_ = bf16[32,6,8,1024]{3,2,1,0:T(8,128)(2,1)} custom-call(bf16[2,256,512]{2,1,0:T(8,128)(2,1)S(1)} %get-tuple-element.41.refs_0_, bf16[2,256,512]{2,1,0:T(8,128)(2,1)S(1)} %get-tuple-element.42.refs_1_, bf16[6,8,64,128]{3,2,1,0:T(8,128)(2,1)S(1)} %get-tuple-element.43.refs_2_, ...), custom_call_target="tpu_custom_call", output_to_operand_aliasing={{}: (10, {})} | custom-call | tf_op jit(solution)/shard_map/update/pallas_call | solution.py:430
  123.1 1.6 %update.7 = bf16[32,6,8,1024]{3,2,1,0:T(8,128)(2,1)} custom-call(bf16[2,256,512]{2,1,0:T(8,128)(2,1)S(1)} %get-tuple-element.41.refs_0_, bf16[2,256,512]{2,1,0:T(8,128)(2,1)S(1)} %get-tuple-element.42.refs_1_, bf16[6,8,64,128]{3,2,1,0:T(8,128)(2,1)S(1)} %get-tuple-element.43.refs_2_, ...), custom_call_target="tpu_custom_call", output_to_operand_aliasing={{}: (10, {})} | custom-call | tf_op jit(solution)/shard_map/update/pallas_call | solution.py:430
  (54 shorter events, 0.9 us)
Async XLA Ops:
  4.1 17.2 %collective-permute-start.7 = (bf16[6,4,8,1024]{3,2,1,0:T(8,128)(2,1)}, bf16[6,4,8,1024]{3,2,1,0:T(8,128)(2,1)S(1)}, u32[]{:S(2)}, u32[]{:S(2)}) collective-permute-start(bf16[6,4,8,1024]{3,2,1,0:T(8,128)(2,1)} %get-tuple-element.35), channel_id=1, source_target_pairs={{0,1},{1,0},{2,3},{3,2},{4,5},{5,4},{6,7},{7,6},{8,9},{9,8},{10,11... | collective-permute-start | bytes 1179656 | tf_op jit(solution)/shard_map/ppermute | solution.py:456
  4.8 11.4 %copy-start.4 = (s32[8,1,128]{2,1,0:T(1,128)S(1)}, s32[8,1,128]{2,1,0:T(1,128)}, u32[]{:S(2)}) copy-start(s32[8,1,128]{2,1,0:T(1,128)} %param.10) | copy-start | bytes 12292
  4.8 11.4 %copy-start = (f32[32,12]{0,1:T(8,128)S(1)}, f32[32,12]{0,1:T(8,128)}, u32[]{:S(2)}) copy-start(f32[32,12]{0,1:T(8,128)} %param.8) | copy-start | bytes 4612
  4.8 11.4 %copy-start.1 = (f32[8,1,128]{2,1,0:T(1,128)S(1)}, f32[8,1,128]{2,1,0:T(1,128)}, u32[]{:S(2)}) copy-start(f32[8,1,128]{2,1,0:T(1,128)} %param.12) | copy-start | bytes 12292
  4.8 11.4 %copy-start.2 = (f32[8,1,128]{2,1,0:T(1,128)S(1)}, f32[8,1,128]{2,1,0:T(1,128)}, u32[]{:S(2)}) copy-start(f32[8,1,128]{2,1,0:T(1,128)} %param.11) | copy-start | bytes 12292
  4.8 16.2 %copy-start.5 = (s32[8]{0:T(128)S(1)}, s32[8]{0:T(128)}, u32[]{:S(2)}) copy-start(s32[8]{0:T(128)} %param.13) | copy-start | bytes 100
  4.8 22.8 %copy-start.3 = (s32[12,6]{0,1:T(8,128)S(1)}, s32[12,6]{0,1:T(8,128)}, u32[]{:S(2)}) copy-start(s32[12,6]{0,1:T(8,128)} %param.9) | copy-start | bytes 868
  4.8 19.9 %collective-permute-start.8 = (bf16[6,4,8,1024]{3,2,1,0:T(8,128)(2,1)}, bf16[6,4,8,1024]{3,2,1,0:T(8,128)(2,1)S(1)}, u32[]{:S(2)}, u32[]{:S(2)}) collective-permute-start(bf16[6,4,8,1024]{3,2,1,0:T(8,128)(2,1)} %get-tuple-element.36), channel_id=1, source_target_pairs={{1,2},{3,4},{5,6},{7,8},{9,10},{11,12},{13,14},{2,1},{4,3},{6,5},{... | collective-permute-start | bytes 1179656 | tf_op jit(solution)/shard_map/ppermute | solution.py:461
  15.8 9.1 %collective-permute-start.5 = (bf16[6,4,8,1024]{3,2,1,0:T(8,128)(2,1)}, bf16[6,4,8,1024]{3,2,1,0:T(8,128)(2,1)S(1)}, u32[]{:S(2)}, u32[]{:S(2)}) collective-permute-start(bf16[6,4,8,1024]{3,2,1,0:T(8,128)(2,1)} %get-tuple-element.32), channel_id=1, source_target_pairs={{0,1},{1,0},{2,3},{3,2},{4,5},{5,4},{6,7},{7,6},{8,9},{9,8},{10,11... | collective-permute-start | bytes 1179656 | tf_op jit(solution)/shard_map/ppermute | solution.py:456
  16.2 5.0 %collective-permute-start.2 = (f32[40,128]{1,0:T(8,128)S(1)}, f32[40,128]{1,0:T(8,128)S(1)}, u32[]{:S(2)}, u32[]{:S(2)}) collective-permute-start(f32[40,128]{1,0:T(8,128)S(1)} %select_maximum_fusion.refs_4_), channel_id=1, source_target_pairs={{16,0},{0,16},{17,1},{1,17},{18,2},{2,18},{19,3},{3,19},{20,4},{4,... | collective-permute-start | bytes 61448 | tf_op jit(solution)/shard_map/ppermute | solution.py:448
  17.5 21.9 %collective-permute-start.6 = (bf16[6,4,8,1024]{3,2,1,0:T(8,128)(2,1)}, bf16[6,4,8,1024]{3,2,1,0:T(8,128)(2,1)S(1)}, u32[]{:S(2)}, u32[]{:S(2)}) collective-permute-start(bf16[6,4,8,1024]{3,2,1,0:T(8,128)(2,1)} %get-tuple-element.33), channel_id=1, source_target_pairs={{1,2},{3,4},{5,6},{7,8},{9,10},{11,12},{13,14},{2,1},{4,3},{6,5},{... | collective-permute-start | bytes 1179656 | tf_op jit(solution)/shard_map/ppermute | solution.py:461
  21.2 23.8 %collective-permute-start.3 = (bf16[6,4,8,1024]{3,2,1,0:T(8,128)(2,1)}, bf16[6,4,8,1024]{3,2,1,0:T(8,128)(2,1)S(1)}, u32[]{:S(2)}, u32[]{:S(2)}) collective-permute-start(bf16[6,4,8,1024]{3,2,1,0:T(8,128)(2,1)} %get-tuple-element.30), channel_id=1, source_target_pairs={{0,1},{1,0},{2,3},{3,2},{4,5},{5,4},{6,7},{7,6},{8,9},{9,8},{10,11... | collective-permute-start | bytes 1179656 | tf_op jit(solution)/shard_map/ppermute | solution.py:456
  21.3 23.8 %collective-permute-start.4 = (bf16[6,4,8,1024]{3,2,1,0:T(8,128)(2,1)}, bf16[6,4,8,1024]{3,2,1,0:T(8,128)(2,1)S(1)}, u32[]{:S(2)}, u32[]{:S(2)}) collective-permute-start(bf16[6,4,8,1024]{3,2,1,0:T(8,128)(2,1)} %get-tuple-element.31), channel_id=1, source_target_pairs={{1,2},{3,4},{5,6},{7,8},{9,10},{11,12},{13,14},{2,1},{4,3},{6,5},{... | collective-permute-start | bytes 1179656 | tf_op jit(solution)/shard_map/ppermute | solution.py:461
  24.8 25.8 %collective-permute-start = (bf16[6,4,8,1024]{3,2,1,0:T(8,128)(2,1)}, bf16[6,4,8,1024]{3,2,1,0:T(8,128)(2,1)S(1)}, u32[]{:S(2)}, u32[]{:S(2)}) collective-permute-start(bf16[6,4,8,1024]{3,2,1,0:T(8,128)(2,1)} %get-tuple-element.28), channel_id=1, source_target_pairs={{0,1},{1,0},{2,3},{3,2},{4,5},{5,4},{6,7},{7,6},{8,9},{9,8},{10,11... | collective-permute-start | bytes 1179656 | tf_op jit(solution)/shard_map/ppermute | solution.py:456
  24.9 25.7 %collective-permute-start.1 = (bf16[6,4,8,1024]{3,2,1,0:T(8,128)(2,1)}, bf16[6,4,8,1024]{3,2,1,0:T(8,128)(2,1)S(1)}, u32[]{:S(2)}, u32[]{:S(2)}) collective-permute-start(bf16[6,4,8,1024]{3,2,1,0:T(8,128)(2,1)} %get-tuple-element.29), channel_id=1, source_target_pairs={{1,2},{3,4},{5,6},{7,8},{9,10},{11,12},{13,14},{2,1},{4,3},{6,5},{... | collective-permute-start | bytes 1179656 | tf_op jit(solution)/shard_map/ppermute | solution.py:461
  56.1 5.6 %collective-permute-start.9 = (bf16[4,8,2,8,128]{4,3,2,1,0:T(8,128)(2,1)S(1)}, bf16[4,8,2,8,128]{4,3,2,1,0:T(8,128)(2,1)S(1)}, u32[]{:S(2)}, u32[]{:S(2)}) collective-permute-start(bf16[4,8,2,8,128]{4,3,2,1,0:T(8,128)(2,1)S(1)} %get-tuple-element.40), channel_id=1, source_target_pairs={{16,0},{0,16},{17,1},{1,17},{18,2},{2,18},{19,3},{3,19},{20,4},{4,... | collective-permute-start | bytes 393224 | tf_op jit(solution)/shard_map/ppermute | solution.py:448
  56.5 54.0 %collective-permute-start.14 = (bf16[6,8,64,128]{3,2,1,0:T(8,128)(2,1)S(1)}, bf16[6,8,64,128]{3,2,1,0:T(8,128)(2,1)S(1)}, u32[]{:S(2)}, u32[]{:S(2)}) collective-permute-start(bf16[6,8,64,128]{3,2,1,0:T(8,128)(2,1)S(1)} %get-tuple-element.45.refs_4_), channel_id=1, source_target_pairs={{16,0},{0,16},{17,1},{1,17},{18,2},{2,18},{19,3},{3,19},{20,4},{4,... | collective-permute-start | bytes 2359304 | tf_op jit(solution)/shard_map/ppermute | solution.py:448
  57.7 52.5 %collective-permute-start.17 = (bf16[4,8,64,128]{3,2,1,0:T(8,128)(2,1)S(1)}, bf16[4,8,64,128]{3,2,1,0:T(8,128)(2,1)S(1)}, u32[]{:S(2)}, u32[]{:S(2)}) collective-permute-start(bf16[4,8,64,128]{3,2,1,0:T(8,128)(2,1)S(1)} %get-tuple-element.48.refs_3_), channel_id=1, source_target_pairs={{16,0},{0,16},{17,1},{1,17},{18,2},{2,18},{19,3},{3,19},{20,4},{4,... | collective-permute-start | bytes 1572872 | tf_op jit(solution)/shard_map/ppermute | solution.py:448
  57.9 54.4 %collective-permute-start.12 = (bf16[6,8,64,128]{3,2,1,0:T(8,128)(2,1)S(1)}, bf16[6,8,64,128]{3,2,1,0:T(8,128)(2,1)S(1)}, u32[]{:S(2)}, u32[]{:S(2)}) collective-permute-start(bf16[6,8,64,128]{3,2,1,0:T(8,128)(2,1)S(1)} %get-tuple-element.43.refs_2_), channel_id=1, source_target_pairs={{16,0},{0,16},{17,1},{1,17},{18,2},{2,18},{19,3},{3,19},{20,4},{4,... | collective-permute-start | bytes 2359304 | tf_op jit(solution)/shard_map/ppermute | solution.py:448
  63.8 1.4 %collective-permute-start.10 = (bf16[8,1,72,128]{3,2,1,0:T(8,128)(2,1)S(1)}, bf16[8,1,72,128]{3,2,1,0:T(8,128)(2,1)S(1)}, u32[]{:S(2)}, u32[]{:S(2)}) collective-permute-start(bf16[8,1,72,128]{3,2,1,0:T(8,128)(2,1)S(1)} %get-tuple-element.60), channel_id=1, source_target_pairs={{0,1},{1,0},{2,3},{3,2},{4,5},{5,4},{6,7},{7,6},{8,9},{9,8},{10,11... | collective-permute-start | bytes 442376 | tf_op jit(solution)/shard_map/ppermute | solution.py:456
  64.0 44.7 %collective-permute-start.19 = (bf16[2,8,64,128]{3,2,1,0:T(8,128)(2,1)S(1)}, bf16[2,8,64,128]{3,2,1,0:T(8,128)(2,1)S(1)}, u32[]{:S(2)}, u32[]{:S(2)}) collective-permute-start(bf16[2,8,64,128]{3,2,1,0:T(8,128)(2,1)S(1)} %get-tuple-element.50.refs_5_), channel_id=1, source_target_pairs={{16,0},{0,16},{17,1},{1,17},{18,2},{2,18},{19,3},{3,19},{20,4},{4,... | collective-permute-start | bytes 786440 | tf_op jit(solution)/shard_map/ppermute | solution.py:448
  65.3 8.7 %collective-permute-start.11 = (bf16[8,1,72,128]{3,2,1,0:T(8,128)(2,1)S(1)}, bf16[8,1,72,128]{3,2,1,0:T(8,128)(2,1)S(1)}, u32[]{:S(2)}, u32[]{:S(2)}) collective-permute-start(bf16[8,1,72,128]{3,2,1,0:T(8,128)(2,1)S(1)} %get-tuple-element.60), channel_id=1, source_target_pairs={{1,2},{3,4},{5,6},{7,8},{9,10},{11,12},{13,14},{2,1},{4,3},{6,5},{... | collective-permute-start | bytes 442376 | tf_op jit(solution)/shard_map/ppermute | solution.py:461
  80.1 1.2 collective-permute-start.20
  81.3 2.9 %collective-permute-start.21 = (f32[12,32]{1,0:T(8,128)S(1)}, f32[12,32]{1,0:T(8,128)S(1)}, u32[]{:S(2)}, u32[]{:S(2)}) collective-permute-start(f32[12,32]{1,0:T(8,128)S(1)} %add.42), channel_id=1, source_target_pairs={{0,2},{1,3},{2,0},{3,1},{4,6},{5,7},{6,4},{7,5},{8,10},{9,11},{10,... | collective-permute-start | bytes 4616 | tf_op jit(solution)/shard_map/ppermute | solution.py:558
  84.2 2.8 %collective-permute-start.22 = (f32[12,32]{1,0:T(8,128)S(1)}, f32[12,32]{1,0:T(8,128)S(1)}, u32[]{:S(2)}, u32[]{:S(2)}) collective-permute-start(f32[12,32]{1,0:T(8,128)S(1)} %add.43), channel_id=1, source_target_pairs={{0,4},{1,5},{2,6},{3,7},{4,0},{5,1},{6,2},{7,3},{8,12},{9,13},{10,... | collective-permute-start | bytes 4616 | tf_op jit(solution)/shard_map/ppermute | solution.py:558
  87.0 22.0 %collective-permute-start.23 = (f32[12,32]{1,0:T(8,128)S(1)}, f32[12,32]{1,0:T(8,128)S(1)}, u32[]{:S(2)}, u32[]{:S(2)}) collective-permute-start(f32[12,32]{1,0:T(8,128)S(1)} %add.44), channel_id=1, source_target_pairs={{0,8},{1,9},{2,10},{3,11},{4,12},{5,13},{6,14},{7,15},{8,0},{9,1},... | collective-permute-start | bytes 4616 | tf_op jit(solution)/shard_map/ppermute | solution.py:558
  108.7 8.3 %collective-permute-start.18 = (bf16[2,8,64,128]{3,2,1,0:T(8,128)(2,1)S(1)}, bf16[2,8,64,128]{3,2,1,0:T(8,128)(2,1)S(1)}, u32[]{:S(2)}, u32[]{:S(2)}) collective-permute-start(bf16[2,8,64,128]{3,2,1,0:T(8,128)(2,1)S(1)} %get-tuple-element.49.refs_5_), channel_id=1, source_target_pairs={{16,0},{0,16},{17,1},{1,17},{18,2},{2,18},{19,3},{3,19},{20,4},{4,... | collective-permute-start | bytes 786440 | tf_op jit(solution)/shard_map/ppermute | solution.py:448
  109.0 12.5 %collective-permute-start.13 = (bf16[2,8,64,128]{3,2,1,0:T(8,128)(2,1)S(1)}, bf16[2,8,64,128]{3,2,1,0:T(8,128)(2,1)S(1)}, u32[]{:S(2)}, u32[]{:S(2)}) collective-permute-start(bf16[2,8,64,128]{3,2,1,0:T(8,128)(2,1)S(1)} %get-tuple-element.44.refs_3_), channel_id=1, source_target_pairs={{16,0},{0,16},{17,1},{1,17},{18,2},{2,18},{19,3},{3,19},{20,4},{4,... | collective-permute-start | bytes 786440 | tf_op jit(solution)/shard_map/ppermute | solution.py:448
  110.2 11.3 %collective-permute-start.16 = (bf16[1,8,64,128]{3,2,1,0:T(8,128)(2,1)S(1)}, bf16[1,8,64,128]{3,2,1,0:T(8,128)(2,1)S(1)}, u32[]{:S(2)}, u32[]{:S(2)}) collective-permute-start(bf16[1,8,64,128]{3,2,1,0:T(8,128)(2,1)S(1)} %get-tuple-element.47.refs_5_), channel_id=1, source_target_pairs={{16,0},{0,16},{17,1},{1,17},{18,2},{2,18},{19,3},{3,19},{20,4},{4,... | collective-permute-start | bytes 393224 | tf_op jit(solution)/shard_map/ppermute | solution.py:448
  110.5 12.6 %collective-permute-start.15 = (bf16[1,8,64,128]{3,2,1,0:T(8,128)(2,1)S(1)}, bf16[1,8,64,128]{3,2,1,0:T(8,128)(2,1)S(1)}, u32[]{:S(2)}, u32[]{:S(2)}) collective-permute-start(bf16[1,8,64,128]{3,2,1,0:T(8,128)(2,1)S(1)} %get-tuple-element.46.refs_5_), channel_id=1, source_target_pairs={{16,0},{0,16},{17,1},{1,17},{18,2},{2,18},{19,3},{3,19},{20,4},{4,... | collective-permute-start | bytes 393224 | tf_op jit(solution)/shard_map/ppermute | solution.py:448
where the time goes:
time: 125 us
  Pallas kernels  46.9 us (38%)
  waiting for transfers between devices  44.8 us (36%)
  starting transfers between devices  28.5 us (23%)
  matrix products  1.88 us (2%)
  other arithmetic  1.46 us (1%)
    ppermute x10, waiting for transfers between devices, from_member(): lax.ppermute(array, 'member', [((i + shift) % count, i) for i in range(co...  27.9 us
    pallas_call x4, Pallas kernels, stencil(): pl.pallas_call(lambda *refs: stencil_kernel(fields, rows, levels, cols, b...  21 us
    ppermute x5, starting transfers between devices, swap_two(): return lax.ppermute(array, 'slab', pairs + [(j, i) for i, j in pairs])  17.2 us
    ppermute x5, waiting for transfers between devices, swap_two(): return lax.ppermute(array, 'slab', pairs + [(j, i) for i, j in pairs])  11.6 us
    pallas_call x2, Pallas kernels, pack(): pl.pallas_call(lambda *refs: pack_kernel(fields, rows, levels, cols, coun...  11.1 us
    pallas_call x4, Pallas kernels, update(): pl.pallas_call(lambda *refs: update_kernel(members, rows, cols, blocks, o...  8.76 us
    ppermute x10, starting transfers between devices, from_member(): lax.ppermute(array, 'member', [((i + shift) % count, i) for i in range(co...  7.52 us
    pallas_call x1, Pallas kernels, solve(): pl.pallas_call(lambda *refs: solve_kernel(rows, members, ensemble, pairs,...  5.95 us
  transfers between devices with their start and end apart: 24, of which 10 were waited for; matrix products, arithmetic and copies ran while one was open for 3% of the time, Pallas kernels for 29%

commit v1 on v0

--- a/solution.py
+++ b/solution.py
@@ -555,8 +555,11 @@
     part = jnp.einsum("jk,ej->ke", ppert, weight_rows, precision=highest)
     step = 1
     while step < slabs:
-        part = part + lax.ppermute(part, "slab", [(i, i ^ step) for i in range(slabs)])
-        step *= 2
+        ways = min(4, slabs // step)
+        part = sum(
+            (lax.ppermute(part, "slab", [(i, i ^ (k * step)) for i in range(slabs)]) for k in range(1, ways)), part
+        )
+        step *= ways
     total = part / (rows * slabs * devices)
     param_analysis = pbar + total.T
     return (analysis, param_analysis)

time: 125 us -> 130 us (1.040)
  the two profiles are of different devices: /device:TPU:17 before, /device:TPU:1 now
where the time goes in v1:
time: 130 us
  Pallas kernels  46.8 us (36%)
  starting transfers between devices  39.3 us (30%)
  waiting for transfers between devices  37.5 us (29%)
  other arithmetic  2.87 us (2%)
  matrix products  1.88 us (1%)
    ppermute x10, waiting for transfers between devices, from_member(): lax.ppermute(array, 'member', [((i + shift) % count, i) for i in range(co...  22.4 us
    pallas_call x4, Pallas kernels, stencil(): pl.pallas_call(lambda *refs: stencil_kernel(fields, rows, levels, cols, b...  21 us
    ppermute x5, starting transfers between devices, swap_two(): return lax.ppermute(array, 'slab', pairs + [(j, i) for i, j in pairs])  19.1 us
    ppermute x6, starting transfers between devices, cycle(): lax.ppermute(part, 'slab', [(i, i ^ k * step) for i in range(slabs)])  11.5 us
    pallas_call x2, Pallas kernels, pack(): pl.pallas_call(lambda *refs: pack_kernel(fields, rows, levels, cols, coun...  11.1 us
    pallas_call x4, Pallas kernels, update(): pl.pallas_call(lambda *refs: update_kernel(members, rows, cols, blocks, o...  8.76 us
    ppermute x5, waiting for transfers between devices, swap_two(): return lax.ppermute(array, 'slab', pairs + [(j, i) for i, j in pairs])  8.02 us
    ppermute x10, starting transfers between devices, from_member(): lax.ppermute(array, 'member', [((i + shift) % count, i) for i in range(co...  7.5 us
  transfers between devices with their start and end apart: 26, of which 9 were waited for; matrix products, arithmetic and copies ran while one was open for 3% of the time, Pallas kernels for 31%

profile of v1, /device:TPU:1, one launch (start us, length us, event | category | flops | bytes accessed | tf_op | source)
XLA Modules:
  0.0 129.6 jit_solution(5904615944839066843)
XLA Ops:
  0.6 0.7 convert_bitcast_fusion.1
  1.3 0.7 select_maximum_fusion.refs_4_
  2.0 2.0 %collective-permute-start.2 = (f32[40,128]{1,0:T(8,128)S(1)}, f32[40,128]{1,0:T(8,128)S(1)}, u32[]{:S(2)}, u32[]{:S(2)}) collective-permute-start(f32[40,128]{1,0:T(8,128)S(1)} %select_maximum_fusion.refs_4_), channel_id=1, source_target_pairs={{16,0},{0,16},{17,1},{1,17},{18,2},{2,18},{19,3},{3,19},{20,4},{4,... | collective-permute-start | bytes 61448 | tf_op jit(solution)/shard_map/ppermute | solution.py:448
  4.1 3.4 %pack.3 = (bf16[6,4,8,1024]{3,2,1,0:T(8,128)(2,1)}, bf16[6,4,8,1024]{3,2,1,0:T(8,128)(2,1)}, f32[1,6,8,8,1024]{4,3,2,1,0:T(8,128)S(1)}) custom-call(f32[12288,128]{1,0:T(8,128)} %bitcast.37), custom_call_target="tpu_custom_call" | custom-call | tf_op jit(solution)/shard_map/pack/pallas_call | solution.py:85
  7.5 1.0 collective-permute-start.7
  8.5 3.2 %collective-permute-start.8 = (bf16[6,4,8,1024]{3,2,1,0:T(8,128)(2,1)}, bf16[6,4,8,1024]{3,2,1,0:T(8,128)(2,1)S(1)}, u32[]{:S(2)}, u32[]{:S(2)}) collective-permute-start(bf16[6,4,8,1024]{3,2,1,0:T(8,128)(2,1)} %get-tuple-element.36), channel_id=1, source_target_pairs={{1,2},{3,4},{5,6},{7,8},{9,10},{11,12},{13,14},{2,1},{4,3},{6,5},{... | collective-permute-start | bytes 1179656 | tf_op jit(solution)/shard_map/ppermute | solution.py:461
  11.7 7.7 %pack.2 = (bf16[6,4,8,1024]{3,2,1,0:T(8,128)(2,1)}, bf16[6,4,8,1024]{3,2,1,0:T(8,128)(2,1)}, bf16[6,4,8,1024]{3,2,1,0:T(8,128)(2,1)}, bf16[6,4,8,1024]{3,2,1,0:T...) custom-call(f32[12288,128]{1,0:T(8,128)} %bitcast.38), custom_call_target="tpu_custom_call" | custom-call | tf_op jit(solution)/shard_map/pack/pallas_call | solution.py:85
  19.5 3.5 %collective-permute-start.6 = (bf16[6,4,8,1024]{3,2,1,0:T(8,128)(2,1)}, bf16[6,4,8,1024]{3,2,1,0:T(8,128)(2,1)S(1)}, u32[]{:S(2)}, u32[]{:S(2)}) collective-permute-start(bf16[6,4,8,1024]{3,2,1,0:T(8,128)(2,1)} %get-tuple-element.33), channel_id=1, source_target_pairs={{1,2},{3,4},{5,6},{7,8},{9,10},{11,12},{13,14},{2,1},{4,3},{6,5},{... | collective-permute-start | bytes 1179656 | tf_op jit(solution)/shard_map/ppermute | solution.py:461
  23.1 0.2 fusion.15.refs_3_
  23.6 3.5 %collective-permute-start.4 = (bf16[6,4,8,1024]{3,2,1,0:T(8,128)(2,1)}, bf16[6,4,8,1024]{3,2,1,0:T(8,128)(2,1)S(1)}, u32[]{:S(2)}, u32[]{:S(2)}) collective-permute-start(bf16[6,4,8,1024]{3,2,1,0:T(8,128)(2,1)} %get-tuple-element.31), channel_id=1, source_target_pairs={{1,2},{3,4},{5,6},{7,8},{9,10},{11,12},{13,14},{2,1},{4,3},{6,5},{... | collective-permute-start | bytes 1179656 | tf_op jit(solution)/shard_map/ppermute | solution.py:461
  27.2 3.5 %collective-permute-start.1 = (bf16[6,4,8,1024]{3,2,1,0:T(8,128)(2,1)}, bf16[6,4,8,1024]{3,2,1,0:T(8,128)(2,1)S(1)}, u32[]{:S(2)}, u32[]{:S(2)}) collective-permute-start(bf16[6,4,8,1024]{3,2,1,0:T(8,128)(2,1)} %get-tuple-element.29), channel_id=1, source_target_pairs={{1,2},{3,4},{5,6},{7,8},{9,10},{11,12},{13,14},{2,1},{4,3},{6,5},{... | collective-permute-start | bytes 1179656 | tf_op jit(solution)/shard_map/ppermute | solution.py:461
  30.9 4.4 %stencil.4 = (bf16[6,8,64,128]{3,2,1,0:T(8,128)(2,1)S(1)}, bf16[4,8,2,8,128]{4,3,2,1,0:T(8,128)(2,1)S(1)}) custom-call(f32[1,6,8,8,1024]{4,3,2,1,0:T(8,128)S(1)} %get-tuple-element.34.refs_0_, bf16[6,4,8,1024]{3,2,1,0:T(8,128)(2,1)S(1)} %collective-permute-done.7.refs_1_, bf16[6,4,8,1024]{3,2,1,0:T(8,128)(2,1)S(1)} %collective-permute-done.8.refs_2_, ...), custom_call_target="tpu_custom_call" | custom-call | tf_op jit(solution)/shard_map/stencil/pallas_call | solution.py:252
  35.3 5.4 %collective-permute-done.6.refs_2_ = bf16[6,4,8,1024]{3,2,1,0:T(8,128)(2,1)S(1)} collective-permute-done((bf16[6,4,8,1024]{3,2,1,0:T(8,128)(2,1)}, bf16[6,4,8,1024]{3,2,1,0:T(8,128)(2,1)S(1)}, u32[]{:S(2)}, u32[]{:S(2)}) %collective-permute-start.6) | collective-permute-done | bytes 393248 | tf_op jit(solution)/shard_map/ppermute | solution.py:461
  40.7 5.5 %stencil.5 = (bf16[4,8,64,128]{3,2,1,0:T(8,128)(2,1)S(1)}, bf16[2,8,64,128]{3,2,1,0:T(8,128)(2,1)S(1)}, bf16[4,8,2,8,128]{4,3,2,1,0:T(8,128)(2,1)S(1)}) custom-call(f32[3,6,8,8,1024]{4,3,2,1,0:T(8,128)} %get-tuple-element.27.refs_0_, bf16[6,4,8,1024]{3,2,1,0:T(8,128)(2,1)S(1)} %collective-permute-done.5.refs_1_, ...), custom_call_target="tpu_custom_call", output_to_operand_aliasing={{2}: (6, {})} | custom-call | tf_op jit(solution)/shard_map/stencil/pallas_call | solution.py:252
  46.3 5.5 %stencil.6 = (bf16[6,8,64,128]{3,2,1,0:T(8,128)(2,1)S(1)}, bf16[4,8,2,8,128]{4,3,2,1,0:T(8,128)(2,1)S(1)}) custom-call(f32[3,6,8,8,1024]{4,3,2,1,0:T(8,128)} %get-tuple-element.27.refs_0_, bf16[6,4,8,1024]{3,2,1,0:T(8,128)(2,1)S(1)} %collective-permute-done.3.refs_1_, ...), custom_call_target="tpu_custom_call", output_to_operand_aliasing={{1}: (6, {})} | custom-call | tf_op jit(solution)/shard_map/stencil/pallas_call | solution.py:252
  51.9 5.5 %stencil.7 = (bf16[2,8,64,128]{3,2,1,0:T(8,128)(2,1)S(1)}, bf16[2,8,64,128]{3,2,1,0:T(8,128)(2,1)S(1)}, bf16[1,8,64,128]{3,2,1,0:T(8,128)(2,1)S(1)}, bf16[1,8,64...) custom-call(f32[3,6,8,8,1024]{4,3,2,1,0:T(8,128)} %get-tuple-element.27.refs_0_, ...), custom_call_target="tpu_custom_call", output_to_operand_aliasing={{4}: (6, {})} | custom-call | tf_op jit(solution)/shard_map/stencil/pallas_call | solution.py:252
  57.4 0.3 collective-permute-start.9
  57.7 1.2 collective-permute-start.14
  59.0 0.3 collective-permute-start.17
  59.2 1.2 collective-permute-start.12
  60.4 2.6 %collective-permute-done.9 = bf16[4,8,2,8,128]{4,3,2,1,0:T(8,128)(2,1)S(1)} collective-permute-done((bf16[4,8,2,8,128]{4,3,2,1,0:T(8,128)(2,1)S(1)}, bf16[4,8,2,8,128]{4,3,2,1,0:T(8,128)(2,1)S(1)}, u32[]{:S(2)}, u32[]{:S(2)}) %collective-permute-start.9) | collective-permute-done | bytes 131104 | tf_op jit(solution)/shard_map/ppermute | solution.py:448
  63.4 0.6 fusion
  63.9 0.9 fusion.12
  65.2 5.3 %collective-permute-start.11 = (bf16[8,1,72,128]{3,2,1,0:T(8,128)(2,1)S(1)}, bf16[8,1,72,128]{3,2,1,0:T(8,128)(2,1)S(1)}, u32[]{:S(2)}, u32[]{:S(2)}) collective-permute-start(bf16[8,1,72,128]{3,2,1,0:T(8,128)(2,1)S(1)} %get-tuple-element.60), channel_id=1, source_target_pairs={{1,2},{3,4},{5,6},{7,8},{9,10},{11,12},{13,14},{2,1},{4,3},{6,5},{... | collective-permute-start | bytes 442376 | tf_op jit(solution)/shard_map/ppermute | solution.py:461
  70.6 0.3 collective-permute-start.19
  70.9 2.6 %collective-permute-done.11.refs_3_ = bf16[8,1,72,128]{3,2,1,0:T(8,128)(2,1)S(1)} collective-permute-done((bf16[8,1,72,128]{3,2,1,0:T(8,128)(2,1)S(1)}, bf16[8,1,72,128]{3,2,1,0:T(8,128)(2,1)S(1)}, u32[]{:S(2)}, u32[]{:S(2)}) %collective-permute-start.11) | collective-permute-done | bytes 147488 | tf_op jit(solution)/shard_map/ppermute | solution.py:461
  73.5 5.9 %solve.1 = (bf16[2,256,512]{2,1,0:T(8,128)(2,1)S(1)}, bf16[2,256,512]{2,1,0:T(8,128)(2,1)S(1)}, f32[32,128]{1,0:T(8,128)S(1)}) custom-call(f32[17,8]{1,0:T(8,128)S(1)} %fusion.7.refs_0_, f32[8,1,72,128]{3,2,1,0:T(8,128)S(1)} %get-tuple-element.61.refs_1_, bf16[8,1,72,128]{3,2,1,0:T(8,128)(2,1)S(1)} %collective-permute-done.10.refs_2_, ...), custom_call_target="tpu_custom_call" | custom-call | tf_op jit(solution)/shard_map/solve/pallas_call | solution.py:392
  79.4 0.2 fusion.3
  79.7 1.2 collective-permute-done.20
  80.8 2.4 %collective-permute-start.21 = (f32[12,32]{1,0:T(8,128)S(1)}, f32[12,32]{1,0:T(8,128)S(1)}, u32[]{:S(2)}, u32[]{:S(2)}) collective-permute-start(f32[12,32]{1,0:T(8,128)S(1)} %fusion.3), channel_id=1, source_target_pairs={{0,2},{1,3},{2,0},{3,1},{4,6},{5,7},{6,4},{7,5},{8,10},{9,11},{10,... | collective-permute-start | bytes 4616 | tf_op jit(solution)/shard_map/ppermute | solution.py:560
  83.3 1.3 %collective-permute-done.21 = f32[12,32]{1,0:T(8,128)S(1)} collective-permute-done((f32[12,32]{1,0:T(8,128)S(1)}, f32[12,32]{1,0:T(8,128)S(1)}, u32[]{:S(2)}, u32[]{:S(2)}) %collective-permute-start.21) | collective-permute-done | bytes 1568 | tf_op jit(solution)/shard_map/ppermute | solution.py:560
  84.6 2.4 %collective-permute-start.22 = (f32[12,32]{1,0:T(8,128)S(1)}, f32[12,32]{1,0:T(8,128)S(1)}, u32[]{:S(2)}, u32[]{:S(2)}) collective-permute-start(f32[12,32]{1,0:T(8,128)S(1)} %fusion.3), channel_id=1, source_target_pairs={{0,3},{1,2},{2,1},{3,0},{4,7},{5,6},{6,5},{7,4},{8,11},{9,10},{10,... | collective-permute-start | bytes 4616 | tf_op jit(solution)/shard_map/ppermute | solution.py:560
  87.0 1.6 %collective-permute-done.22 = f32[12,32]{1,0:T(8,128)S(1)} collective-permute-done((f32[12,32]{1,0:T(8,128)S(1)}, f32[12,32]{1,0:T(8,128)S(1)}, u32[]{:S(2)}, u32[]{:S(2)}) %collective-permute-start.22) | collective-permute-done | bytes 1568 | tf_op jit(solution)/shard_map/ppermute | solution.py:560
  88.6 1.3 %collective-permute-start.23 = (f32[12,32]{1,0:T(8,128)S(1)}, f32[12,32]{1,0:T(8,128)S(1)}, u32[]{:S(2)}, u32[]{:S(2)}) collective-permute-start(f32[12,32]{1,0:T(8,128)S(1)} %add_add_fusion), channel_id=1, source_target_pairs={{0,4},{1,5},{2,6},{3,7},{4,0},{5,1},{6,2},{7,3},{8,12},{9,13},{10,... | collective-permute-start | bytes 4616 | tf_op jit(solution)/shard_map/ppermute | solution.py:560
  89.9 16.3 %collective-permute-done.19.refs_9_ = bf16[2,8,64,128]{3,2,1,0:T(8,128)(2,1)S(1)} collective-permute-done((bf16[2,8,64,128]{3,2,1,0:T(8,128)(2,1)S(1)}, bf16[2,8,64,128]{3,2,1,0:T(8,128)(2,1)S(1)}, u32[]{:S(2)}, u32[]{:S(2)}) %collective-permute-start.19) | collective-permute-done | bytes 262176 | tf_op jit(solution)/shard_map/ppermute | solution.py:448
  106.3 4.3 %collective-permute-start.24 = (f32[12,32]{1,0:T(8,128)S(1)}, f32[12,32]{1,0:T(8,128)S(1)}, u32[]{:S(2)}, u32[]{:S(2)}) collective-permute-start(f32[12,32]{1,0:T(8,128)S(1)} %add_add_fusion), channel_id=1, source_target_pairs={{0,8},{1,9},{2,10},{3,11},{4,12},{5,13},{6,14},{7,15},{8,0},{9,1},... | collective-permute-start | bytes 4616 | tf_op jit(solution)/shard_map/ppermute | solution.py:560
  110.6 1.1 collective-permute-start.25
  111.6 0.3 collective-permute-start.18
  112.0 2.9 %collective-permute-done.25 = f32[12,32]{1,0:T(8,128)S(1)} collective-permute-done((f32[12,32]{1,0:T(8,128)S(1)}, f32[12,32]{1,0:T(8,128)S(1)}, u32[]{:S(2)}, u32[]{:S(2)}) %collective-permute-start.25) | collective-permute-done | bytes 1568 | tf_op jit(solution)/shard_map/ppermute | solution.py:560
  114.9 0.3 collective-permute-start.13
  115.2 1.1 collective-permute-start.16
  116.3 0.3 collective-permute-start.15
  116.7 0.7 add_bitcast_fusion
  117.3 2.8 %update.4.refs_10_ = bf16[32,6,8,1024]{3,2,1,0:T(8,128)(2,1)} custom-call(bf16[2,256,512]{2,1,0:T(8,128)(2,1)S(1)} %get-tuple-element.41.refs_0_, bf16[2,256,512]{2,1,0:T(8,128)(2,1)S(1)} %get-tuple-element.42.refs_1_, bf16[6,8,64,128]{3,2,1,0:T(8,128)(2,1)S(1)} %get-tuple-element.43.refs_2_, bf16[4,8,64,128]{3,2,1,0:T(8,128)(2,1)S(1)} %get-tuple-element.48.refs_3_, ...), custom_call_target="tpu_custom_call" | custom-call | tf_op jit(solution)/shard_map/update/pallas_call | solution.py:430
  120.1 2.8 %update.5.refs_10_ = bf16[32,6,8,1024]{3,2,1,0:T(8,128)(2,1)} custom-call(bf16[2,256,512]{2,1,0:T(8,128)(2,1)S(1)} %get-tuple-element.41.refs_0_, bf16[2,256,512]{2,1,0:T(8,128)(2,1)S(1)} %get-tuple-element.42.refs_1_, bf16[6,8,64,128]{3,2,1,0:T(8,128)(2,1)S(1)} %get-tuple-element.43.refs_2_, ...), custom_call_target="tpu_custom_call", output_to_operand_aliasing={{}: (10, {})} | custom-call | tf_op jit(solution)/shard_map/update/pallas_call | solution.py:430
  122.9 3.5 %collective-permute-done.16.refs_9_ = bf16[1,8,64,128]{3,2,1,0:T(8,128)(2,1)S(1)} collective-permute-done((bf16[1,8,64,128]{3,2,1,0:T(8,128)(2,1)S(1)}, bf16[1,8,64,128]{3,2,1,0:T(8,128)(2,1)S(1)}, u32[]{:S(2)}, u32[]{:S(2)}) %collective-permute-start.16) | collective-permute-done | bytes 131104 | tf_op jit(solution)/shard_map/ppermute | solution.py:448
  126.4 1.6 %update.6.refs_10_ = bf16[32,6,8,1024]{3,2,1,0:T(8,128)(2,1)} custom-call(bf16[2,256,512]{2,1,0:T(8,128)(2,1)S(1)} %get-tuple-element.41.refs_0_, bf16[2,256,512]{2,1,0:T(8,128)(2,1)S(1)} %get-tuple-element.42.refs_1_, bf16[6,8,64,128]{3,2,1,0:T(8,128)(2,1)S(1)} %get-tuple-element.43.refs_2_, ...), custom_call_target="tpu_custom_call", output_to_operand_aliasing={{}: (10, {})} | custom-call | tf_op jit(solution)/shard_map/update/pallas_call | solution.py:430
  128.0 1.6 %update.7 = bf16[32,6,8,1024]{3,2,1,0:T(8,128)(2,1)} custom-call(bf16[2,256,512]{2,1,0:T(8,128)(2,1)S(1)} %get-tuple-element.41.refs_0_, bf16[2,256,512]{2,1,0:T(8,128)(2,1)S(1)} %get-tuple-element.42.refs_1_, bf16[6,8,64,128]{3,2,1,0:T(8,128)(2,1)S(1)} %get-tuple-element.43.refs_2_, ...), custom_call_target="tpu_custom_call", output_to_operand_aliasing={{}: (10, {})} | custom-call | tf_op jit(solution)/shard_map/update/pallas_call | solution.py:430
  (54 shorter events, 1.3 us)
Async XLA Ops:
  2.0 21.5 %collective-permute-start.2 = (f32[40,128]{1,0:T(8,128)S(1)}, f32[40,128]{1,0:T(8,128)S(1)}, u32[]{:S(2)}, u32[]{:S(2)}) collective-permute-start(f32[40,128]{1,0:T(8,128)S(1)} %select_maximum_fusion.refs_4_), channel_id=1, source_target_pairs={{16,0},{0,16},{17,1},{1,17},{18,2},{2,18},{19,3},{3,19},{20,4},{4,... | collective-permute-start | bytes 61448 | tf_op jit(solution)/shard_map/ppermute | solution.py:448
  7.5 16.1 %collective-permute-start.7 = (bf16[6,4,8,1024]{3,2,1,0:T(8,128)(2,1)}, bf16[6,4,8,1024]{3,2,1,0:T(8,128)(2,1)S(1)}, u32[]{:S(2)}, u32[]{:S(2)}) collective-permute-start(bf16[6,4,8,1024]{3,2,1,0:T(8,128)(2,1)} %get-tuple-element.35), channel_id=1, source_target_pairs={{0,1},{1,0},{2,3},{3,2},{4,5},{5,4},{6,7},{7,6},{8,9},{9,8},{10,11... | collective-permute-start | bytes 1179656 | tf_op jit(solution)/shard_map/ppermute | solution.py:456
  8.5 14.6 %copy-start.4 = (s32[8]{0:T(128)S(1)}, s32[8]{0:T(128)}, u32[]{:S(2)}) copy-start(s32[8]{0:T(128)} %param.13) | copy-start | bytes 100
  8.5 14.6 %copy-start = (f32[32,12]{0,1:T(8,128)S(1)}, f32[32,12]{0,1:T(8,128)}, u32[]{:S(2)}) copy-start(f32[32,12]{0,1:T(8,128)} %param.8) | copy-start | bytes 4612
  8.5 14.6 %copy-start.3 = (s32[12,6]{0,1:T(8,128)S(1)}, s32[12,6]{0,1:T(8,128)}, u32[]{:S(2)}) copy-start(s32[12,6]{0,1:T(8,128)} %param.9) | copy-start | bytes 868
  8.5 18.6 %collective-permute-start.8 = (bf16[6,4,8,1024]{3,2,1,0:T(8,128)(2,1)}, bf16[6,4,8,1024]{3,2,1,0:T(8,128)(2,1)S(1)}, u32[]{:S(2)}, u32[]{:S(2)}) collective-permute-start(bf16[6,4,8,1024]{3,2,1,0:T(8,128)(2,1)} %get-tuple-element.36), channel_id=1, source_target_pairs={{1,2},{3,4},{5,6},{7,8},{9,10},{11,12},{13,14},{2,1},{4,3},{6,5},{... | collective-permute-start | bytes 1179656 | tf_op jit(solution)/shard_map/ppermute | solution.py:461
  19.4 7.7 %collective-permute-start.5 = (bf16[6,4,8,1024]{3,2,1,0:T(8,128)(2,1)}, bf16[6,4,8,1024]{3,2,1,0:T(8,128)(2,1)S(1)}, u32[]{:S(2)}, u32[]{:S(2)}) collective-permute-start(bf16[6,4,8,1024]{3,2,1,0:T(8,128)(2,1)} %get-tuple-element.32), channel_id=1, source_target_pairs={{0,1},{1,0},{2,3},{3,2},{4,5},{5,4},{6,7},{7,6},{8,9},{9,8},{10,11... | collective-permute-start | bytes 1179656 | tf_op jit(solution)/shard_map/ppermute | solution.py:456
  19.5 21.2 %collective-permute-start.6 = (bf16[6,4,8,1024]{3,2,1,0:T(8,128)(2,1)}, bf16[6,4,8,1024]{3,2,1,0:T(8,128)(2,1)S(1)}, u32[]{:S(2)}, u32[]{:S(2)}) collective-permute-start(bf16[6,4,8,1024]{3,2,1,0:T(8,128)(2,1)} %get-tuple-element.33), channel_id=1, source_target_pairs={{1,2},{3,4},{5,6},{7,8},{9,10},{11,12},{13,14},{2,1},{4,3},{6,5},{... | collective-permute-start | bytes 1179656 | tf_op jit(solution)/shard_map/ppermute | solution.py:461
  23.5 22.7 %collective-permute-start.3 = (bf16[6,4,8,1024]{3,2,1,0:T(8,128)(2,1)}, bf16[6,4,8,1024]{3,2,1,0:T(8,128)(2,1)S(1)}, u32[]{:S(2)}, u32[]{:S(2)}) collective-permute-start(bf16[6,4,8,1024]{3,2,1,0:T(8,128)(2,1)} %get-tuple-element.30), channel_id=1, source_target_pairs={{0,1},{1,0},{2,3},{3,2},{4,5},{5,4},{6,7},{7,6},{8,9},{9,8},{10,11... | collective-permute-start | bytes 1179656 | tf_op jit(solution)/shard_map/ppermute | solution.py:456
  23.6 22.7 %collective-permute-start.4 = (bf16[6,4,8,1024]{3,2,1,0:T(8,128)(2,1)}, bf16[6,4,8,1024]{3,2,1,0:T(8,128)(2,1)S(1)}, u32[]{:S(2)}, u32[]{:S(2)}) collective-permute-start(bf16[6,4,8,1024]{3,2,1,0:T(8,128)(2,1)} %get-tuple-element.31), channel_id=1, source_target_pairs={{1,2},{3,4},{5,6},{7,8},{9,10},{11,12},{13,14},{2,1},{4,3},{6,5},{... | collective-permute-start | bytes 1179656 | tf_op jit(solution)/shard_map/ppermute | solution.py:461
  27.1 24.7 %collective-permute-start = (bf16[6,4,8,1024]{3,2,1,0:T(8,128)(2,1)}, bf16[6,4,8,1024]{3,2,1,0:T(8,128)(2,1)S(1)}, u32[]{:S(2)}, u32[]{:S(2)}) collective-permute-start(bf16[6,4,8,1024]{3,2,1,0:T(8,128)(2,1)} %get-tuple-element.28), channel_id=1, source_target_pairs={{0,1},{1,0},{2,3},{3,2},{4,5},{5,4},{6,7},{7,6},{8,9},{9,8},{10,11... | collective-permute-start | bytes 1179656 | tf_op jit(solution)/shard_map/ppermute | solution.py:456
  27.2 24.7 %collective-permute-start.1 = (bf16[6,4,8,1024]{3,2,1,0:T(8,128)(2,1)}, bf16[6,4,8,1024]{3,2,1,0:T(8,128)(2,1)S(1)}, u32[]{:S(2)}, u32[]{:S(2)}) collective-permute-start(bf16[6,4,8,1024]{3,2,1,0:T(8,128)(2,1)} %get-tuple-element.29), channel_id=1, source_target_pairs={{1,2},{3,4},{5,6},{7,8},{9,10},{11,12},{13,14},{2,1},{4,3},{6,5},{... | collective-permute-start | bytes 1179656 | tf_op jit(solution)/shard_map/ppermute | solution.py:461
  51.8 11.3 %copy-start.1 = (f32[8,1,128]{2,1,0:T(1,128)S(1)}, f32[8,1,128]{2,1,0:T(1,128)}, u32[]{:S(2)}) copy-start(f32[8,1,128]{2,1,0:T(1,128)} %param.12) | copy-start | bytes 12292
  51.9 11.3 %copy-start.2 = (f32[8,1,128]{2,1,0:T(1,128)S(1)}, f32[8,1,128]{2,1,0:T(1,128)}, u32[]{:S(2)}) copy-start(f32[8,1,128]{2,1,0:T(1,128)} %param.11) | copy-start | bytes 12292
  57.4 5.6 %collective-permute-start.9 = (bf16[4,8,2,8,128]{4,3,2,1,0:T(8,128)(2,1)S(1)}, bf16[4,8,2,8,128]{4,3,2,1,0:T(8,128)(2,1)S(1)}, u32[]{:S(2)}, u32[]{:S(2)}) collective-permute-start(bf16[4,8,2,8,128]{4,3,2,1,0:T(8,128)(2,1)S(1)} %get-tuple-element.40), channel_id=1, source_target_pairs={{16,0},{0,16},{17,1},{1,17},{18,2},{2,18},{19,3},{3,19},{20,4},{4,... | collective-permute-start | bytes 393224 | tf_op jit(solution)/shard_map/ppermute | solution.py:448
  57.7 58.6 %collective-permute-start.14 = (bf16[6,8,64,128]{3,2,1,0:T(8,128)(2,1)S(1)}, bf16[6,8,64,128]{3,2,1,0:T(8,128)(2,1)S(1)}, u32[]{:S(2)}, u32[]{:S(2)}) collective-permute-start(bf16[6,8,64,128]{3,2,1,0:T(8,128)(2,1)S(1)} %get-tuple-element.45.refs_4_), channel_id=1, source_target_pairs={{16,0},{0,16},{17,1},{1,17},{18,2},{2,18},{19,3},{3,19},{20,4},{4,... | collective-permute-start | bytes 2359304 | tf_op jit(solution)/shard_map/ppermute | solution.py:448
  59.0 56.2 %collective-permute-start.17 = (bf16[4,8,64,128]{3,2,1,0:T(8,128)(2,1)S(1)}, bf16[4,8,64,128]{3,2,1,0:T(8,128)(2,1)S(1)}, u32[]{:S(2)}, u32[]{:S(2)}) collective-permute-start(bf16[4,8,64,128]{3,2,1,0:T(8,128)(2,1)S(1)} %get-tuple-element.48.refs_3_), channel_id=1, source_target_pairs={{16,0},{0,16},{17,1},{1,17},{18,2},{2,18},{19,3},{3,19},{20,4},{4,... | collective-permute-start | bytes 1572872 | tf_op jit(solution)/shard_map/ppermute | solution.py:448
  59.2 58.1 %collective-permute-start.12 = (bf16[6,8,64,128]{3,2,1,0:T(8,128)(2,1)S(1)}, bf16[6,8,64,128]{3,2,1,0:T(8,128)(2,1)S(1)}, u32[]{:S(2)}, u32[]{:S(2)}) collective-permute-start(bf16[6,8,64,128]{3,2,1,0:T(8,128)(2,1)S(1)} %get-tuple-element.43.refs_2_), channel_id=1, source_target_pairs={{16,0},{0,16},{17,1},{1,17},{18,2},{2,18},{19,3},{3,19},{20,4},{4,... | collective-permute-start | bytes 2359304 | tf_op jit(solution)/shard_map/ppermute | solution.py:448
  65.2 5.4 %collective-permute-start.10 = (bf16[8,1,72,128]{3,2,1,0:T(8,128)(2,1)S(1)}, bf16[8,1,72,128]{3,2,1,0:T(8,128)(2,1)S(1)}, u32[]{:S(2)}, u32[]{:S(2)}) collective-permute-start(bf16[8,1,72,128]{3,2,1,0:T(8,128)(2,1)S(1)} %get-tuple-element.60), channel_id=1, source_target_pairs={{0,1},{1,0},{2,3},{3,2},{4,5},{5,4},{6,7},{7,6},{8,9},{9,8},{10,11... | collective-permute-start | bytes 442376 | tf_op jit(solution)/shard_map/ppermute | solution.py:456
  65.2 8.3 %collective-permute-start.11 = (bf16[8,1,72,128]{3,2,1,0:T(8,128)(2,1)S(1)}, bf16[8,1,72,128]{3,2,1,0:T(8,128)(2,1)S(1)}, u32[]{:S(2)}, u32[]{:S(2)}) collective-permute-start(bf16[8,1,72,128]{3,2,1,0:T(8,128)(2,1)S(1)} %get-tuple-element.60), channel_id=1, source_target_pairs={{1,2},{3,4},{5,6},{7,8},{9,10},{11,12},{13,14},{2,1},{4,3},{6,5},{... | collective-permute-start | bytes 442376 | tf_op jit(solution)/shard_map/ppermute | solution.py:461
  70.6 35.7 %collective-permute-start.19 = (bf16[2,8,64,128]{3,2,1,0:T(8,128)(2,1)S(1)}, bf16[2,8,64,128]{3,2,1,0:T(8,128)(2,1)S(1)}, u32[]{:S(2)}, u32[]{:S(2)}) collective-permute-start(bf16[2,8,64,128]{3,2,1,0:T(8,128)(2,1)S(1)} %get-tuple-element.50.refs_5_), channel_id=1, source_target_pairs={{16,0},{0,16},{17,1},{1,17},{18,2},{2,18},{19,3},{3,19},{20,4},{4,... | collective-permute-start | bytes 786440 | tf_op jit(solution)/shard_map/ppermute | solution.py:448
  79.6 1.2 collective-permute-start.20
  80.8 3.8 %collective-permute-start.21 = (f32[12,32]{1,0:T(8,128)S(1)}, f32[12,32]{1,0:T(8,128)S(1)}, u32[]{:S(2)}, u32[]{:S(2)}) collective-permute-start(f32[12,32]{1,0:T(8,128)S(1)} %fusion.3), channel_id=1, source_target_pairs={{0,2},{1,3},{2,0},{3,1},{4,6},{5,7},{6,4},{7,5},{8,10},{9,11},{10,... | collective-permute-start | bytes 4616 | tf_op jit(solution)/shard_map/ppermute | solution.py:560
  84.6 4.0 %collective-permute-start.22 = (f32[12,32]{1,0:T(8,128)S(1)}, f32[12,32]{1,0:T(8,128)S(1)}, u32[]{:S(2)}, u32[]{:S(2)}) collective-permute-start(f32[12,32]{1,0:T(8,128)S(1)} %fusion.3), channel_id=1, source_target_pairs={{0,3},{1,2},{2,1},{3,0},{4,7},{5,6},{6,5},{7,4},{8,11},{9,10},{10,... | collective-permute-start | bytes 4616 | tf_op jit(solution)/shard_map/ppermute | solution.py:560
  88.6 21.9 %collective-permute-start.23 = (f32[12,32]{1,0:T(8,128)S(1)}, f32[12,32]{1,0:T(8,128)S(1)}, u32[]{:S(2)}, u32[]{:S(2)}) collective-permute-start(f32[12,32]{1,0:T(8,128)S(1)} %add_add_fusion), channel_id=1, source_target_pairs={{0,4},{1,5},{2,6},{3,7},{4,0},{5,1},{6,2},{7,3},{8,12},{9,13},{10,... | collective-permute-start | bytes 4616 | tf_op jit(solution)/shard_map/ppermute | solution.py:560
  106.3 5.4 %collective-permute-start.24 = (f32[12,32]{1,0:T(8,128)S(1)}, f32[12,32]{1,0:T(8,128)S(1)}, u32[]{:S(2)}, u32[]{:S(2)}) collective-permute-start(f32[12,32]{1,0:T(8,128)S(1)} %add_add_fusion), channel_id=1, source_target_pairs={{0,8},{1,9},{2,10},{3,11},{4,12},{5,13},{6,14},{7,15},{8,0},{9,1},... | collective-permute-start | bytes 4616 | tf_op jit(solution)/shard_map/ppermute | solution.py:560
  110.6 4.3 %collective-permute-start.25 = (f32[12,32]{1,0:T(8,128)S(1)}, f32[12,32]{1,0:T(8,128)S(1)}, u32[]{:S(2)}, u32[]{:S(2)}) collective-permute-start(f32[12,32]{1,0:T(8,128)S(1)} %add_add_fusion), channel_id=1, source_target_pairs={{0,12},{1,13},{2,14},{3,15},{4,8},{5,9},{6,10},{7,11},{8,4},{9,5},... | collective-permute-start | bytes 4616 | tf_op jit(solution)/shard_map/ppermute | solution.py:560
  111.6 8.5 %collective-permute-start.18 = (bf16[2,8,64,128]{3,2,1,0:T(8,128)(2,1)S(1)}, bf16[2,8,64,128]{3,2,1,0:T(8,128)(2,1)S(1)}, u32[]{:S(2)}, u32[]{:S(2)}) collective-permute-start(bf16[2,8,64,128]{3,2,1,0:T(8,128)(2,1)S(1)} %get-tuple-element.49.refs_5_), channel_id=1, source_target_pairs={{16,0},{0,16},{17,1},{1,17},{18,2},{2,18},{19,3},{3,19},{20,4},{4,... | collective-permute-start | bytes 786440 | tf_op jit(solution)/shard_map/ppermute | solution.py:448
  114.9 11.5 %collective-permute-start.13 = (bf16[2,8,64,128]{3,2,1,0:T(8,128)(2,1)S(1)}, bf16[2,8,64,128]{3,2,1,0:T(8,128)(2,1)S(1)}, u32[]{:S(2)}, u32[]{:S(2)}) collective-permute-start(bf16[2,8,64,128]{3,2,1,0:T(8,128)(2,1)S(1)} %get-tuple-element.44.refs_3_), channel_id=1, source_target_pairs={{16,0},{0,16},{17,1},{1,17},{18,2},{2,18},{19,3},{3,19},{20,4},{4,... | collective-permute-start | bytes 786440 | tf_op jit(solution)/shard_map/ppermute | solution.py:448
  115.2 11.2 %collective-permute-start.16 = (bf16[1,8,64,128]{3,2,1,0:T(8,128)(2,1)S(1)}, bf16[1,8,64,128]{3,2,1,0:T(8,128)(2,1)S(1)}, u32[]{:S(2)}, u32[]{:S(2)}) collective-permute-start(bf16[1,8,64,128]{3,2,1,0:T(8,128)(2,1)S(1)} %get-tuple-element.47.refs_5_), channel_id=1, source_target_pairs={{16,0},{0,16},{17,1},{1,17},{18,2},{2,18},{19,3},{3,19},{20,4},{4,... | collective-permute-start | bytes 393224 | tf_op jit(solution)/shard_map/ppermute | solution.py:448
  116.3 11.7 %collective-permute-start.15 = (bf16[1,8,64,128]{3,2,1,0:T(8,128)(2,1)S(1)}, bf16[1,8,64,128]{3,2,1,0:T(8,128)(2,1)S(1)}, u32[]{:S(2)}, u32[]{:S(2)}) collective-permute-start(bf16[1,8,64,128]{3,2,1,0:T(8,128)(2,1)S(1)} %get-tuple-element.46.refs_5_), channel_id=1, source_target_pairs={{16,0},{0,16},{17,1},{1,17},{18,2},{2,18},{19,3},{3,19},{20,4},{4,... | collective-permute-start | bytes 393224 | tf_op jit(solution)/shard_map/ppermute | solution.py:448
